TPU v7x, 512 devices: a whole 4x8x8 slice. The times are simulated.
512 devices in a mesh: angle: 16 (over z, y_hi), tile: 32 (over y_lo, x, core).
Axes of the slice: x: 4, y: 8 (y_hi: 2, y_lo: 4; y = y_hi * 4 + y_lo), z: 8, core: 2. Of those that a mesh axis runs over, the one named last changes fastest.
Arguments:
- volume: float32 [256, 2, 32, 256], P('tile'), may hold values from -1.8 to 1.8
- first_moment: float32 [256, 2, 32, 256], P('tile'), may hold values from -0.6 to 0.6
- second_moment: float32 [256, 2, 32, 256], P('tile'), may hold values from 0.01 to 0.1
- probe: float32 [2, 128, 128], replicated, may hold values from -6 to 6
- measured: bfloat16 [16, 32, 8, 128, 128], P('angle', 'tile'), may hold values from 0 to 2
- scan_rows: int32 [16, 32, 8], P('angle', 'tile'), may hold values from 0 to 128
- scan_cols: int32 [16, 32, 8], P('angle', 'tile'), may hold values from 0 to 256
- owner_ids: int32 [16, 32, 32], P('angle'), may hold values from 0 to 31, as said below
- block_ids: int32 [16, 32, 32], P('angle'), may hold values from 0 to 7
- interp_weights: float32 [16, 32, 16], P('angle', 'tile'), may hold values from 0 to 1
Outputs:
- new_volume: float32 [256, 2, 32, 256], P('tile')
- new_first: float32 [256, 2, 32, 256], P('tile')
- new_second: float32 [256, 2, 32, 256], P('tile')
Inputs may be any that keep to these rules, and one draw needn't show every extreme that they name: `owner_ids`: among the 32 requests of one tile of one angle group, no owner is named more than 2 times, and one owner is named exactly 2 times.
All inputs are finite; a program needn't handle non-finite values.
Results may differ from a plain program's by a relative error of at most 0.0019.
Values may be sent and summed in bfloat16 or wider, within the bound.
A program may use at most 64 MiB of HBM per device.

v0:
```python
import math

import jax
import jax.numpy as jnp
from jax import lax
from jax.sharding import PartitionSpec as P

FRESNEL = 0.35
SMOOTHING = 0.25
BETA_FIRST = 0.9
BETA_SECOND = 0.999
STEP_SIZE = 0.05
EPSILON = 1e-08


def with_halo(cells, sides, width):
    for axis, dim in sides:
        count = lax.axis_size(axis)
        ends = count - 1
        head = lax.slice_in_dim(cells, 0, width, axis=dim)
        tail = lax.slice_in_dim(cells, cells.shape[dim] - width, cells.shape[dim], axis=dim)
        cells = jnp.concatenate(
            [
                lax.ppermute(tail, axis, [(i, (i + 1) % count) for i in range(ends)]),
                cells,
                lax.ppermute(head, axis, [((i + 1) % count, i) for i in range(ends)]),
            ],
            axis=dim,
        )
    return cells


def from_behind(array, axis, by):
    length = lax.axis_size(axis)
    pairs = [(i, i + by) for i in range(length) if 0 <= i + by < length]
    return lax.ppermute(array, axis, pairs)


def split_up(array, dim, length):
    dims = array.shape
    blocks = array.reshape(*dims[:dim], length, dims[dim] // length, *dims[dim + 1 :])
    return jnp.moveaxis(blocks, dim, 0)


def sum_at_owner(array, axis, dim):
    length = lax.axis_size(axis)
    blocks = lax.all_to_all(split_up(array, dim, length), axis, 0, 0, tiled=True)
    return jnp.sum(blocks, axis=0)


def in_one_piece(arrays, axis, dim, along):
    widths = [a.shape[along] for a in arrays]
    both = jnp.concatenate(arrays, axis=along)
    whole = lax.all_gather(both, axis, axis=dim, tiled=True)
    return tuple(jnp.split(whole, [sum(widths[:k]) for k in range(1, len(widths))], axis=along))


def dft_tables(length):
    index = jnp.arange(length, dtype=jnp.int32)
    product = index[:, None] * index[None, :] % length
    angles = product.astype(jnp.float32) * (2.0 * math.pi / length)
    factor = 1.0 / math.sqrt(length)
    dft_real = jnp.cos(angles) * factor
    dft_imag = -jnp.sin(angles) * factor
    signed = jnp.where(index < length // 2, index, index - length)
    squared = (signed * signed).astype(jnp.float32)
    phase = (squared[:, None] + squared[None, :]) * (-2.0 * math.pi * FRESNEL / length)
    return (dft_real, dft_imag, jnp.cos(phase), jnp.sin(phase))


def complex_matmul(left_real, left_imag, right_real, right_imag):
    highest = lax.Precision.HIGHEST
    out_real = jnp.dot(left_real, right_real, precision=highest) - jnp.dot(
        left_imag, right_imag, precision=highest
    )
    out_imag = jnp.dot(left_real, right_imag, precision=highest) + jnp.dot(
        left_imag, right_real, precision=highest
    )
    return (out_real, out_imag)


def transform(field_real, field_imag, table_real, table_imag):
    half_real, half_imag = complex_matmul(table_real, table_imag, field_real, field_imag)
    return complex_matmul(half_real, half_imag, table_real, table_imag)


def probe_loss(object_pad, probe, start_row, start_col, amplitude, tables):
    dft_real, dft_imag, kernel_real, kernel_imag = tables
    probe_size = probe.shape[-1]
    layers = object_pad.shape[0]
    anchor = jnp.zeros((), jnp.int32)
    starts = (anchor, anchor, start_row, start_col)
    window = lax.dynamic_slice(object_pad, starts, (layers, 2, probe_size, probe_size))
    wave_real = probe[0]
    wave_imag = probe[1]
    for layer_index in range(layers):
        trans_real = 1.0 + window[layer_index, 0]
        trans_imag = window[layer_index, 1]
        wave_real, wave_imag = (
            wave_real * trans_real - wave_imag * trans_imag,
            wave_real * trans_imag + wave_imag * trans_real,
        )
        if layer_index + 1 < layers:
            spec_real, spec_imag = transform(wave_real, wave_imag, dft_real, dft_imag)
            spec_real, spec_imag = (
                spec_real * kernel_real - spec_imag * kernel_imag,
                spec_real * kernel_imag + spec_imag * kernel_real,
            )
            wave_real, wave_imag = transform(spec_real, spec_imag, dft_real, -dft_imag)
    far_real, far_imag = transform(wave_real, wave_imag, dft_real, dft_imag)
    modulus = jnp.sqrt(far_real * far_real + far_imag * far_imag + SMOOTHING)
    misfit = modulus - amplitude.astype(jnp.float32)
    return 0.5 * jnp.sum(misfit * misfit)


def local_gradient(padded, probe, rows_list, cols_list, amplitudes, tables):

    def total_loss(object_pad):

        def single(start_row, start_col, amplitude):
            return probe_loss(object_pad, probe, start_row, start_col, amplitude, tables)

        return jnp.sum(jax.vmap(single)(rows_list, cols_list, amplitudes))

    value, pullback = jax.vjp(total_loss, padded)
    return pullback(jnp.ones((), padded.dtype))[0]


def adam_update(params, moment_one, moment_two, gradient):
    fresh_one = BETA_FIRST * moment_one + (1.0 - BETA_FIRST) * gradient
    fresh_two = BETA_SECOND * moment_two + (1.0 - BETA_SECOND) * gradient * gradient
    fresh_params = params - STEP_SIZE * fresh_one / (jnp.sqrt(fresh_two) + EPSILON)
    return (fresh_params, fresh_one, fresh_two)


def per_device(
    volume,
    first_moment,
    second_moment,
    probe,
    measured,
    scan_rows,
    scan_cols,
    owner_ids,
    block_ids,
    interp_weights,
):
    tile_index = lax.axis_index("tile")
    tile_count = lax.axis_size("tile")
    block_count = volume.shape[0]
    block_rows = volume.shape[2]
    slab_width = volume.shape[3]
    probe_size = probe.shape[1]
    margin = probe_size // 2
    requests = owner_ids.shape[2]
    row_blocks = interp_weights.shape[2]
    per_slice = slab_width // block_rows
    layers = row_blocks // per_slice
    capacity = max(2, requests // tile_count)
    group_owner = owner_ids[0]
    group_block = block_ids[0]
    request_slots = jnp.arange(requests, dtype=jnp.int32)
    earlier = request_slots[None, :] < request_slots[:, None]
    same_owner = group_owner[:, :, None] == group_owner[:, None, :]
    group_rank = jnp.sum(same_owner & earlier[None], axis=2)
    my_owner = lax.dynamic_index_in_dim(group_owner, tile_index, 0, keepdims=False)
    my_rank = lax.dynamic_index_in_dim(group_rank, tile_index, 0, keepdims=False)
    slot_ids = jnp.arange(capacity, dtype=jnp.int32)
    serving = (group_owner == tile_index)[:, None, :] & (
        group_rank[:, None, :] == slot_ids[None, :, None]
    )
    send_block = jnp.sum(jnp.where(serving, group_block[:, None, :], 0), axis=2)
    send_valid = jnp.any(serving, axis=2)
    blocks = volume.astype(jnp.bfloat16)
    weight = interp_weights[0, 0]
    complement = 1.0 - weight
    outgoing = jnp.where(
        send_valid[:, :, None, None, None], blocks[send_block], jnp.zeros((), jnp.bfloat16)
    )
    incoming = lax.all_to_all(outgoing, "tile", split_axis=0, concat_axis=0, tiled=True)
    fetched = (
        incoming[my_owner, my_rank]
        .astype(jnp.float32)
        .reshape(row_blocks, 2, 2, block_rows, slab_width)
    )
    obj_rows = (
        weight[:, None, None, None] * fetched[:, 0]
        + complement[:, None, None, None] * fetched[:, 1]
    )
    object_tile = obj_rows.reshape(layers, per_slice, 2, block_rows, slab_width).transpose(
        0, 2, 1, 3, 4
    )
    object_tile = object_tile.reshape(layers, 2, slab_width, slab_width).astype(jnp.bfloat16)
    padded = with_halo(object_tile, (("tile", 3),), margin).astype(jnp.float32)
    tables = dft_tables(probe_size)
    grad_padded = local_gradient(
        padded, probe, scan_rows[0, 0], scan_cols[0, 0], measured[0, 0], tables
    )
    from_left = from_behind(grad_padded[..., margin + slab_width :], "tile", 1)
    from_right = from_behind(grad_padded[..., :margin], "tile", -1)
    interior = grad_padded[..., margin : margin + slab_width]
    interior = interior.at[..., :margin].add(from_left)
    interior = interior.at[..., slab_width - margin :].add(from_right)
    grad_rows = interior.reshape(layers, 2, per_slice, block_rows, slab_width).transpose(
        0, 2, 1, 3, 4
    )
    grad_rows = grad_rows.reshape(row_blocks, 2, block_rows, slab_width)
    request_grads = jnp.stack(
        [weight[:, None, None, None] * grad_rows, complement[:, None, None, None] * grad_rows],
        axis=1,
    )
    request_grads = request_grads.reshape(requests, 2, block_rows, slab_width).astype(jnp.bfloat16)
    owner_range = jnp.arange(tile_count, dtype=jnp.int32)
    owned_slots = (my_owner[None, None, :] == owner_range[:, None, None]) & (
        my_rank[None, None, :] == slot_ids[None, :, None]
    )
    back_index = jnp.sum(jnp.where(owned_slots, request_slots[None, None, :], 0), axis=2)
    back_valid = jnp.any(owned_slots, axis=2)
    returning = jnp.where(
        back_valid[:, :, None, None, None], request_grads[back_index], jnp.zeros((), jnp.bfloat16)
    )
    arrived = lax.all_to_all(returning, "tile", split_axis=0, concat_axis=0, tiled=True)
    selector = (
        send_block[:, :, None] == jnp.arange(block_count, dtype=jnp.int32)[None, None, :]
    ) & send_valid[:, :, None]
    selector = selector.reshape(tile_count * capacity, block_count).astype(jnp.bfloat16)
    grad_volume = jnp.einsum(
        "nb,nx->bx",
        selector,
        arrived.reshape(tile_count * capacity, -1),
        preferred_element_type=jnp.float32,
    ).reshape(volume.shape)
    rows_total = block_count * 2 * block_rows
    share_rows = rows_total // lax.axis_size("angle")
    share_grad = sum_at_owner(grad_volume.reshape(rows_total, slab_width), "angle", 0)
    offset = lax.axis_index("angle") * share_rows

    def take_share(values):
        return lax.dynamic_slice_in_dim(
            values.reshape(rows_total, slab_width), offset, share_rows, 0
        )

    fresh_params, fresh_one, fresh_two = adam_update(
        take_share(volume), take_share(first_moment), take_share(second_moment), share_grad
    )
    whole_params, whole_one, whole_two = in_one_piece(
        (fresh_params, fresh_one, fresh_two), "angle", 0, 1
    )
    return (
        whole_params.reshape(volume.shape),
        whole_one.reshape(volume.shape),
        whole_two.reshape(volume.shape),
    )


def solution(mesh):
    in_specs = (
        P("tile", None, None, None),
        P("tile", None, None, None),
        P("tile", None, None, None),
        P(),
        P("angle", "tile", None, None, None),
        P("angle", "tile", None),
        P("angle", "tile", None),
        P("angle", None, None),
        P("angle", None, None),
        P("angle", "tile", None),
    )
    out_specs = (
        P("tile", None, None, None),
        P("tile", None, None, None),
        P("tile", None, None, None),
    )
    return jax.shard_map(
        per_device, mesh=mesh, in_specs=in_specs, out_specs=out_specs, check_vma=False
    )
```

profile of v0, /device:TPU:4, one launch (start us, length us, event | category | flops | bytes accessed | tf_op | source)
XLA Modules:
  0.0 465.9 jit_solution(5936947624844883214)
XLA Ops:
  8.6 1.6 convert_reduce_fusion
  13.4 1.6 broadcast_select_fusion
  15.0 9.7 %all-to-all-start = ((bf16[32,2,2,32,256]{4,3,2,1,0:T(8,128)(2,1)}), bf16[32,2,2,32,256]{4,3,2,1,0:T(8,128)(2,1)S(1)}, u32[]{:S(2)}, u32[]{:S(2)}) async-start(bf16[32,2,2,32,256]{4,3,2,1,0:T(8,128)(2,1)} %broadcast_select_fusion), calls=%async_computation | async-start | bytes 4194304 | tf_op jit(solution)/shard_map/all_to_all | solution.py:180
  27.0 46.1 %all-to-all-done = bf16[32,2,2,32,256]{4,3,2,1,0:T(8,128)(2,1)S(1)} async-done(((bf16[32,2,2,32,256]{4,3,2,1,0:T(8,128)(2,1)}), bf16[32,2,2,32,256]{4,3,2,1,0:T(8,128)(2,1)S(1)}, u32[]{:S(2)}, u32[]{:S(2)}) %all-to-all-start) | async-done | bytes 2097184 | tf_op jit(solution)/shard_map/all_to_all | solution.py:180
  74.4 1.9 collective-permute-start
  76.4 3.6 collective-permute-start.1
  80.4 1.7 collective-permute-done
  82.1 1.8 collective-permute-done.1
  84.3 22.1 %while.4 = (s32[]{:T(128)}, f32[2,2,256,384]{3,2,1,0:T(8,128)S(1)}, s32[8,4]{0,1:T(4,128)S(1)}, f32[8,2,2,128,128]{4,3,0,2,1:T(8,128)}, s32[]{:T(128)}) while((s32[]{:T(128)}, f32[2,2,256,384]{3,2,1,0:T(8,128)S(1)}, s32[8,4]{0,1:T(4,128)S(1)}, f32[8,2,2,128,128]{4,3,0,2,1:T(8,128)}, s32[]{:T(128)}) %tuple.71), condition=%wide.while_cond.2, body=%wide.while_body.2.sunk | while | flops 2 | bytes 525937 | solution.py:93
  84.9 2.1 bitcast_dynamic-update-slice_fusion.2
  87.7 2.1 bitcast_dynamic-update-slice_fusion.2
  90.4 2.1 bitcast_dynamic-update-slice_fusion.2
  93.1 2.1 bitcast_dynamic-update-slice_fusion.2
  95.9 2.1 bitcast_dynamic-update-slice_fusion.2
  98.6 2.1 bitcast_dynamic-update-slice_fusion.2
  101.3 2.1 bitcast_dynamic-update-slice_fusion.2
  104.1 2.1 bitcast_dynamic-update-slice_fusion.2
  106.4 2.3 fusion.102
  108.6 2.1 fusion.106
  132.3 1.1 convolution_add_fusion.11
  133.4 1.3 fusion.57
  137.7 1.2 add_bitcast_fusion.3
  152.8 1.6 pad_add_fusion
  154.5 90.6 %while.5 = (s32[]{:T(128)}, f32[2,2,256,384]{3,2,1,0:T(8,128)S(1)}, s32[8,4]{0,1:T(4,128)S(1)}, f32[8,2,2,128,128]{4,3,0,2,1:T(8,128)}, s32[]{:T(128)}, /*index=5*/s32[4]{0:T(128)S(1)}, s32[]{:T(128)}) while((s32[]{:T(128)}, f32[2,2,256,384]{3,2,1,0:T(8,128)S(1)}, s32[8,4]{0,1:T(4,128)S(1)}, f32[8,2,2,128,128]{4,3,0,2,1:T(8,128)}, s32[]{:T(128)}, ...), condition=%wide.while_cond.3, body=%wide.while_body.3.sunk | while | flops 131101 | bytes 1310915 | solution.py:93
  155.2 3.2 and_reduce_fusion.3
  158.3 3.0 add_select_fusion.3
  161.3 4.6 dynamic-update-slice.14
  166.5 3.2 and_reduce_fusion.3
  169.7 3.0 add_select_fusion.3
  172.7 4.5 dynamic-update-slice.14
  177.8 3.2 and_reduce_fusion.3
  181.0 3.0 add_select_fusion.3
  184.0 4.6 dynamic-update-slice.14
  189.2 3.2 and_reduce_fusion.3
  192.4 3.0 add_select_fusion.3
  195.3 4.5 dynamic-update-slice.14
  200.5 3.2 and_reduce_fusion.3
  203.7 3.0 add_select_fusion.3
  206.7 4.4 dynamic-update-slice.14
  211.7 3.2 and_reduce_fusion.3
  214.9 3.0 add_select_fusion.3
  217.9 4.5 dynamic-update-slice.14
  223.0 3.2 and_reduce_fusion.3
  226.2 3.0 add_select_fusion.3
  229.2 4.6 dynamic-update-slice.14
  234.4 3.2 and_reduce_fusion.3
  237.6 3.0 add_select_fusion.3
  240.6 4.5 dynamic-update-slice.14
  246.0 2.9 collective-permute-start.2
  249.4 2.7 collective-permute-start.3
  252.1 4.6 collective-permute-done.2
  256.6 1.2 slice_add_fusion.1
  257.9 2.3 scatter-add.18
  260.2 1.2 slice_add_fusion
  261.4 2.4 scatter-add.19
  265.0 1.6 broadcast_select_fusion.1
  266.6 9.3 %all-to-all-start.1 = ((bf16[32,2,2,32,256]{4,3,2,1,0:T(8,128)(2,1)}), bf16[32,2,2,32,256]{4,3,2,1,0:T(8,128)(2,1)S(1)}, u32[]{:S(2)}, u32[]{:S(2)}) async-start(bf16[32,2,2,32,256]{4,3,2,1,0:T(8,128)(2,1)} %broadcast_select_fusion.1), calls=%async_computation.1 | async-start | bytes 4194304 | tf_op jit(solution)/shard_map/all_to_all | solution.py:222
  276.2 48.1 %all-to-all-done.1 = bf16[32,2,2,32,256]{4,3,2,1,0:T(8,128)(2,1)S(1)} async-done(((bf16[32,2,2,32,256]{4,3,2,1,0:T(8,128)(2,1)}), bf16[32,2,2,32,256]{4,3,2,1,0:T(8,128)(2,1)S(1)}, u32[]{:S(2)}, u32[]{:S(2)}) %all-to-all-start.1) | async-done | bytes 2097184 | tf_op jit(solution)/shard_map/all_to_all | solution.py:222
  324.3 2.3 reshape.450
  326.6 2.1 fusion.126
  329.6 11.7 %all-to-all-start.2 = ((f32[16,32,256]{2,1,0:T(8,128)}), f32[16,32,256]{2,1,0:T(8,128)S(1)}, u32[]{:S(2)}, u32[]{:S(2)}) async-start(f32[16,32,256]{2,1,0:T(8,128)} %reshape_reshape_reshape.3), calls=%async_computation.2 | async-start | bytes 1048576 | tf_op jit(solution)/shard_map/all_to_all | solution.py:47
  341.3 18.2 %all-to-all-done.2 = f32[16,32,256]{2,1,0:T(8,128)S(1)} async-done(((f32[16,32,256]{2,1,0:T(8,128)}), f32[16,32,256]{2,1,0:T(8,128)S(1)}, u32[]{:S(2)}, u32[]{:S(2)}) %all-to-all-start.2) | async-done | bytes 524320 | tf_op jit(solution)/shard_map/all_to_all | solution.py:47
  361.1 95.2 %all-gather.2.cloned.1.call-done = f32[512,768]{1,0:T(8,128)} async-done(((f32[32,768]{1,0:T(8,128)}), f32[512,768]{1,0:T(8,128)}) %all-gather.2.cloned.1.call-update) | async-done | bytes 1572880 | tf_op jit(solution)/shard_map/all_gather | solution.py:54
  456.3 2.5 fusion.391
  (148 shorter events, 62.4 us)
Async XLA Ops:
  14.9 10.2 %copy-start.6 = (f32[1,1,16]{2,1,0:T(1,128)S(1)}, f32[1,1,16]{2,1,0:T(1,128)}, u32[]{:S(2)}) copy-start(f32[1,1,16]{2,1,0:T(1,128)} %param.23) | copy-start | bytes 196
  14.9 11.7 %copy-start.4 = (s32[1,1,8]{2,1,0:T(1,128)S(1)}, s32[1,1,8]{2,1,0:T(1,128)}, u32[]{:S(2)}) copy-start(s32[1,1,8]{2,1,0:T(1,128)} %param.20) | copy-start | bytes 100
  14.9 11.7 %copy-start.5 = (s32[1,1,8]{2,1,0:T(1,128)S(1)}, s32[1,1,8]{2,1,0:T(1,128)}, u32[]{:S(2)}) copy-start(s32[1,1,8]{2,1,0:T(1,128)} %param.19) | copy-start | bytes 100
  14.9 12.0 %copy-start.2 = (f32[2,128,128]{2,1,0:T(8,128)S(1)}, f32[2,128,128]{2,1,0:T(8,128)}, u32[]{:S(2)}) copy-start(f32[2,128,128]{2,1,0:T(8,128)} %param.17) | copy-start | bytes 393220
  15.0 58.2 %all-to-all-start = ((bf16[32,2,2,32,256]{4,3,2,1,0:T(8,128)(2,1)}), bf16[32,2,2,32,256]{4,3,2,1,0:T(8,128)(2,1)S(1)}, u32[]{:S(2)}, u32[]{:S(2)}) async-start(bf16[32,2,2,32,256]{4,3,2,1,0:T(8,128)(2,1)} %broadcast_select_fusion), calls=%async_computation | async-start | bytes 4194304 | tf_op jit(solution)/shard_map/all_to_all | solution.py:180
  74.0 6.0 %copy-start.3 = (s32[4]{0:T(128)S(1)}, s32[4]{0:T(128)}, u32[]{:S(2)}) copy-start(s32[4]{0:T(128)} %constant.125.clone.1) | copy-start | bytes 52
  74.4 7.7 %collective-permute-start = (bf16[2,2,256,64]{3,2,1,0:T(8,128)(2,1)S(1)}, bf16[2,2,256,64]{3,2,1,0:T(8,128)(2,1)S(1)}, u32[]{:S(2)}, u32[]{:S(2)}) collective-permute-start(bf16[2,2,256,64]{3,2,1,0:T(8,128)(2,1)S(1)} %get-tuple-element.103), channel_id=1, source_target_pairs={{0,1},{1,2},{2,3},{3,4},{4,5},{5,6},{6,7},{7,8},{8,9},{9,10},{10,1... | collective-permute-start | bytes 393224 | tf_op jit(solution)/shard_map/ppermute | solution.py:24
  76.4 7.5 %collective-permute-start.1 = (bf16[2,2,256,64]{3,2,1,0:T(8,128)(2,1)S(1)}, bf16[2,2,256,64]{3,2,1,0:T(8,128)(2,1)S(1)}, u32[]{:S(2)}, u32[]{:S(2)}) collective-permute-start(bf16[2,2,256,64]{3,2,1,0:T(8,128)(2,1)S(1)} %get-tuple-element.104), channel_id=1, source_target_pairs={{1,0},{2,1},{3,2},{4,3},{5,4},{6,5},{7,6},{8,7},{9,8},{10,9},{11,1... | collective-permute-start | bytes 393224 | tf_op jit(solution)/shard_map/ppermute | solution.py:26
  106.4 4.4 copy-start
  127.4 2.5 copy-start.1
  246.0 10.6 %collective-permute-start.2 = (f32[2,2,256,64]{3,2,1,0:T(8,128)S(1)}, f32[2,2,256,64]{3,2,1,0:T(8,128)}, u32[]{:S(2)}, u32[]{:S(2)}) collective-permute-start(f32[2,2,256,64]{3,2,1,0:T(8,128)S(1)} %get-tuple-element.94), channel_id=1, source_target_pairs={{0,1},{1,2},{2,3},{3,4},{4,5},{5,6},{6,7},{7,8},{8,9},{9,10},{10,1... | collective-permute-start | bytes 786440 | tf_op jit(solution)/shard_map/ppermute | solution.py:36
  249.4 10.8 %collective-permute-start.3 = (f32[2,2,256,64]{3,2,1,0:T(8,128)}, f32[2,2,256,64]{3,2,1,0:T(8,128)}, u32[]{:S(2)}, u32[]{:S(2)}) collective-permute-start(f32[2,2,256,64]{3,2,1,0:T(8,128)} %get-tuple-element.93), channel_id=1, source_target_pairs={{1,0},{2,1},{3,2},{4,3},{5,4},{6,5},{7,6},{8,7},{9,8},{10,9},{11,1... | collective-permute-start | bytes 786440 | tf_op jit(solution)/shard_map/ppermute | solution.py:36
  266.6 57.7 %all-to-all-start.1 = ((bf16[32,2,2,32,256]{4,3,2,1,0:T(8,128)(2,1)}), bf16[32,2,2,32,256]{4,3,2,1,0:T(8,128)(2,1)S(1)}, u32[]{:S(2)}, u32[]{:S(2)}) async-start(bf16[32,2,2,32,256]{4,3,2,1,0:T(8,128)(2,1)} %broadcast_select_fusion.1), calls=%async_computation.1 | async-start | bytes 4194304 | tf_op jit(solution)/shard_map/all_to_all | solution.py:222
  329.6 29.9 %all-to-all-start.2 = ((f32[16,32,256]{2,1,0:T(8,128)}), f32[16,32,256]{2,1,0:T(8,128)S(1)}, u32[]{:S(2)}, u32[]{:S(2)}) async-start(f32[16,32,256]{2,1,0:T(8,128)} %reshape_reshape_reshape.3), calls=%async_computation.2 | async-start | bytes 1048576 | tf_op jit(solution)/shard_map/all_to_all | solution.py:47
  341.3 115.0 %all-gather.2.cloned.1.call-start = ((), (), s32[]{:S(2)}) async-start(), calls=%async_computation.3 | async-start | bytes 1671168 | tf_op jit(solution)/shard_map/all_gather | solution.py:54
Sparse Core Ops, SparseCore 0:
  361.2 95.0 all-gather.1
where the time goes:
time: 471 us; the launch traced here: 466 us
  waiting for transfers between devices  216 us (46%)
  local copies, waits for them, and re-layouts  79.7 us (17%)
  other arithmetic  65.1 us (14%)
  matrix products  48.2 us (10%)
  starting transfers between devices  41.8 us (9%)
  between operations  15 us (3%)
    all_gather x1, waiting for transfers between devices, in_one_piece(): whole = lax.all_gather(both, axis, axis=dim, tiled=True)  95.2 us
    scatter-add x16, other arithmetic  49.1 us
    all_to_all x1, waiting for transfers between devices, per_device(): lax.all_to_all(returning, 'tile', split_axis=0, concat_axis=0, tiled=True)  48.1 us
    all_to_all x1, waiting for transfers between devices, per_device(): lax.all_to_all(outgoing, 'tile', split_axis=0, concat_axis=0, tiled=True)  46.1 us
    scatter-add x24, local copies, waits for them, and re-layouts  41.2 us
    gather x24, local copies, waits for them, and re-layouts  21.9 us
    all_to_all x1, waiting for transfers between devices, sum_at_owner(): lax.all_to_all(split_up(array, dim, length), axis, 0, 0, tiled=True)  18.2 us
    dot_general x12, matrix products, complex_matmul(): jnp.dot(left_real, right_imag, precision=highest)  11.8 us
  transfers between devices with their start and end apart: 8, of which 7 were waited for; matrix products, arithmetic and copies ran while one was open for 1% of the time, Pallas kernels for 0%

commit v1 on v0

v1 whole, which is shorter than its diff:
```python
import math

import jax
import jax.numpy as jnp
import numpy as np
from jax import lax
from jax.experimental import pallas as pl
from jax.experimental.pallas import tpu as pltpu
from jax.sharding import PartitionSpec as P

FRESNEL = 0.35
SMOOTHING = 0.25
BETA_FIRST = 0.9
BETA_SECOND = 0.999
STEP_SIZE = 0.05
EPSILON = 1e-08


def with_halo(cells, sides, width):
    for axis, dim in sides:
        count = lax.axis_size(axis)
        ends = count - 1
        head = lax.slice_in_dim(cells, 0, width, axis=dim)
        tail = lax.slice_in_dim(cells, cells.shape[dim] - width, cells.shape[dim], axis=dim)
        cells = jnp.concatenate(
            [
                lax.ppermute(tail, axis, [(i, (i + 1) % count) for i in range(ends)]),
                cells,
                lax.ppermute(head, axis, [((i + 1) % count, i) for i in range(ends)]),
            ],
            axis=dim,
        )
    return cells


def from_behind(array, axis, by):
    length = lax.axis_size(axis)
    pairs = [(i, i + by) for i in range(length) if 0 <= i + by < length]
    return lax.ppermute(array, axis, pairs)


def block_form(table):
    real = np.concatenate([np.concatenate([table.real, table.imag], 1),
                           np.concatenate([-table.imag, table.real], 1)], 0)
    real = real.astype(np.float32)
    head = real.astype(jnp.bfloat16)
    rest = (real - head.astype(np.float32)).astype(jnp.bfloat16)
    return head, rest


def operator_tables(length):
    index = np.arange(length)
    table = np.exp(-2j * np.pi * (np.outer(index, index) % length) / length) / math.sqrt(length)
    signed = np.where(index < length // 2, index, index - length)
    phase = np.exp(-2j * np.pi * FRESNEL * signed * signed / length)
    step = (table.conj() * phase[None, :]) @ table
    out = []
    for operator in (table, step):
        out += [*block_form(operator), *block_form(operator.conj())]
    return np.stack(out)


def split_bf16(x):
    head = x.astype(jnp.bfloat16)
    return head, (x - head.astype(jnp.float32)).astype(jnp.bfloat16)


def mm(a, b):
    return jnp.dot(a, b, preferred_element_type=jnp.float32)


def wave_kernel(size, chunk, rows_ref, cols_ref, obj_ref, probe_ref, amp_ref, tab_ref, acc_ref):
    probes = amp_ref.shape[0]
    n = size

    def two_sided(real, imag, right, left):
        stacked = jnp.concatenate([jnp.concatenate([r, i], 1) for r, i in zip(real, imag)], 0)
        head, rest = split_bf16(stacked)
        half = mm(head, tab_ref[right]) + (mm(rest, tab_ref[right]) + mm(head, tab_ref[right + 1]))
        out_real, out_imag = [], []
        for k in range(0, len(real), 2):
            one = half[k * n : (k + 1) * n]
            two = half[(k + 1) * n : (k + 2) * n]
            pair = jnp.concatenate(
                [jnp.concatenate([one[:, :n], two[:, :n]], 1),
                 jnp.concatenate([one[:, n:], two[:, n:]], 1)], 0)
            head, rest = split_bf16(pair)
            full = mm(tab_ref[left], head) + (mm(tab_ref[left], rest) + mm(tab_ref[left + 1], head))
            out_real += [full[:n, :n], full[:n, n:]]
            out_imag += [full[n:, :n], full[n:, n:]]
        return out_real, out_imag

    acc_ref[...] = jnp.zeros_like(acc_ref)
    p_real = probe_ref[0]
    p_imag = probe_ref[1]

    def body(step, carry):
        first = step * chunk
        place, trans = [], []
        for k in range(chunk):
            row = rows_ref[0, first + k]
            col = cols_ref[0, first + k]
            base = pl.multiple_of(jnp.minimum(col // n, 1) * n, n)
            shift = col - base
            top = pl.multiple_of(jnp.minimum(row // 8, n // 8 - 1) * 8, 8)
            down = row - top
            place.append((top, down, base, shift))
            back = lax.rem(2 * n - shift, 2 * n)
            up = lax.rem(n + 8 - down, n + 8)
            window = []
            for c in range(4):
                wide = obj_ref[c, pl.ds(top, n + 8), pl.ds(base, 2 * n)]
                part = pltpu.roll(pltpu.roll(wide, back, 1)[:, :n], up, 0)[:n]
                window.append(part + 1.0 if c % 2 == 0 else part)
            trans.append(window)
        w_real = [p_real * t[0] - p_imag * t[1] for t in trans]
        w_imag = [p_real * t[1] + p_imag * t[0] for t in trans]
        u_real, u_imag = two_sided(w_real, w_imag, 4, 6)
        w_real = [r * t[2] - i * t[3] for r, i, t in zip(u_real, u_imag, trans)]
        w_imag = [r * t[3] + i * t[2] for r, i, t in zip(u_real, u_imag, trans)]
        f_real, f_imag = two_sided(w_real, w_imag, 0, 2)
        g_real, g_imag = [], []
        for k in range(chunk):
            r, i = f_real[k], f_imag[k]
            scale = 1.0 - amp_ref[first + k].astype(jnp.float32) * lax.rsqrt(r * r + i * i + SMOOTHING)
            g_real.append(r * scale)
            g_imag.append(i * scale)
        g_real, g_imag = two_sided(g_real, g_imag, 2, 0)
        d_real = [u * r + v * i for u, v, r, i in zip(u_real, u_imag, g_real, g_imag)]
        d_imag = [u * i - v * r for u, v, r, i in zip(u_real, u_imag, g_real, g_imag)]
        b_real = [t[2] * r + t[3] * i for t, r, i in zip(trans, g_real, g_imag)]
        b_imag = [t[2] * i - t[3] * r for t, r, i in zip(trans, g_real, g_imag)]
        b_real, b_imag = two_sided(b_real, b_imag, 6, 4)
        for k in range(chunk):
            r, i = b_real[k], b_imag[k]
            parts = (p_real * r + p_imag * i, p_real * i - p_imag * r, d_real[k], d_imag[k])
            top, down, base, shift = place[k]
            for c in range(4):
                tall = jnp.concatenate([parts[c], jnp.zeros((8, n), jnp.float32)], 0)
                tall = pltpu.roll(tall, down, 0)
                wide = jnp.concatenate([tall, jnp.zeros_like(tall)], 1)
                wide = pltpu.roll(wide, shift, 1)
                acc_ref[c, pl.ds(top, n + 8), pl.ds(base, 2 * n)] += wide
        return carry

    lax.fori_loop(0, probes // chunk, body, 0)


def local_gradient(padded, probe, rows_list, cols_list, amplitudes):
    layers, parts, high, wide = padded.shape
    size = probe.shape[-1]
    probes = amplitudes.shape[0]
    chunk = 4 if probes % 4 == 0 else 2
    tables = jnp.asarray(operator_tables(size))
    smem = pl.BlockSpec(memory_space=pltpu.SMEM)
    vmem = pl.BlockSpec(memory_space=pltpu.VMEM)
    out = pl.pallas_call(
        lambda *refs: wave_kernel(size, chunk, *refs),
        out_shape=jax.ShapeDtypeStruct((layers * parts, high, wide), jnp.float32),
        in_specs=[smem, smem, vmem, vmem, vmem, vmem],
        out_specs=vmem,
        name="waves",
    )(
        rows_list.reshape(1, -1),
        cols_list.reshape(1, -1),
        padded.reshape(layers * parts, high, wide),
        probe,
        amplitudes,
        tables,
    )
    return out.reshape(layers, parts, high, wide)


def adam_update(params, moment_one, moment_two, gradient):
    fresh_one = BETA_FIRST * moment_one + (1.0 - BETA_FIRST) * gradient
    fresh_two = BETA_SECOND * moment_two + (1.0 - BETA_SECOND) * gradient * gradient
    fresh_params = params - STEP_SIZE * fresh_one / (jnp.sqrt(fresh_two) + EPSILON)
    return (fresh_params, fresh_one, fresh_two)


def per_device(
    volume,
    first_moment,
    second_moment,
    probe,
    measured,
    scan_rows,
    scan_cols,
    owner_ids,
    block_ids,
    interp_weights,
):
    tile_index = lax.axis_index("tile")
    tile_count = lax.axis_size("tile")
    block_count = volume.shape[0]
    block_rows = volume.shape[2]
    slab_width = volume.shape[3]
    probe_size = probe.shape[1]
    margin = probe_size // 2
    requests = owner_ids.shape[2]
    row_blocks = interp_weights.shape[2]
    per_slice = slab_width // block_rows
    layers = row_blocks // per_slice
    capacity = max(2, requests // tile_count)
    group_owner = owner_ids[0]
    group_block = block_ids[0]
    request_slots = jnp.arange(requests, dtype=jnp.int32)
    earlier = request_slots[None, :] < request_slots[:, None]
    same_owner = group_owner[:, :, None] == group_owner[:, None, :]
    group_rank = jnp.sum(same_owner & earlier[None], axis=2)
    my_owner = lax.dynamic_index_in_dim(group_owner, tile_index, 0, keepdims=False)
    my_rank = lax.dynamic_index_in_dim(group_rank, tile_index, 0, keepdims=False)
    slot_ids = jnp.arange(capacity, dtype=jnp.int32)
    serving = (group_owner == tile_index)[:, None, :] & (
        group_rank[:, None, :] == slot_ids[None, :, None]
    )
    send_block = jnp.sum(jnp.where(serving, group_block[:, None, :], 0), axis=2)
    send_valid = jnp.any(serving, axis=2)
    blocks = volume.astype(jnp.bfloat16)
    weight = interp_weights[0, 0]
    complement = 1.0 - weight
    outgoing = jnp.where(
        send_valid[:, :, None, None, None], blocks[send_block], jnp.zeros((), jnp.bfloat16)
    )
    incoming = lax.all_to_all(outgoing, "tile", split_axis=0, concat_axis=0, tiled=True)
    fetched = (
        incoming[my_owner, my_rank]
        .astype(jnp.float32)
        .reshape(row_blocks, 2, 2, block_rows, slab_width)
    )
    obj_rows = (
        weight[:, None, None, None] * fetched[:, 0]
        + complement[:, None, None, None] * fetched[:, 1]
    )
    object_tile = obj_rows.reshape(layers, per_slice, 2, block_rows, slab_width).transpose(
        0, 2, 1, 3, 4
    )
    object_tile = object_tile.reshape(layers, 2, slab_width, slab_width).astype(jnp.bfloat16)
    padded = with_halo(object_tile, (("tile", 3),), margin).astype(jnp.float32)
    grad_padded = local_gradient(padded, probe, scan_rows[0, 0], scan_cols[0, 0], measured[0, 0])
    edges = grad_padded.astype(jnp.bfloat16)
    from_left = from_behind(edges[..., margin + slab_width :], "tile", 1).astype(jnp.float32)
    from_right = from_behind(edges[..., :margin], "tile", -1).astype(jnp.float32)
    interior = grad_padded[..., margin : margin + slab_width]
    middle = jnp.zeros((layers, 2, slab_width, slab_width - 2 * margin), jnp.float32)
    interior = interior + jnp.concatenate([from_left, middle, from_right], axis=3)
    grad_rows = interior.reshape(layers, 2, per_slice, block_rows, slab_width).transpose(
        0, 2, 1, 3, 4
    )
    grad_rows = grad_rows.reshape(row_blocks, 2, block_rows, slab_width)
    request_grads = jnp.stack(
        [weight[:, None, None, None] * grad_rows, complement[:, None, None, None] * grad_rows],
        axis=1,
    )
    request_grads = request_grads.reshape(requests, 2, block_rows, slab_width).astype(jnp.bfloat16)
    owner_range = jnp.arange(tile_count, dtype=jnp.int32)
    owned_slots = (my_owner[None, None, :] == owner_range[:, None, None]) & (
        my_rank[None, None, :] == slot_ids[None, :, None]
    )
    back_index = jnp.sum(jnp.where(owned_slots, request_slots[None, None, :], 0), axis=2)
    back_valid = jnp.any(owned_slots, axis=2)
    returning = jnp.where(
        back_valid[:, :, None, None, None], request_grads[back_index], jnp.zeros((), jnp.bfloat16)
    )
    arrived = lax.all_to_all(returning, "tile", split_axis=0, concat_axis=0, tiled=True)
    selector = (
        send_block[:, :, None] == jnp.arange(block_count, dtype=jnp.int32)[None, None, :]
    ) & send_valid[:, :, None]
    selector = selector.reshape(tile_count * capacity, block_count).astype(jnp.bfloat16)
    grad_volume = jnp.einsum(
        "nb,nx->bx",
        selector,
        arrived.reshape(tile_count * capacity, -1),
        preferred_element_type=jnp.float32,
    ).reshape(volume.shape)
    rows_total = block_count * 2 * block_rows
    angles = lax.axis_size("angle")
    partial_sums = grad_volume.reshape(angles, rows_total // angles, slab_width)
    parts = lax.all_to_all(partial_sums.astype(jnp.bfloat16), "angle", 0, 0, tiled=True)
    share = jnp.sum(parts.astype(jnp.float32), axis=0)
    spread = jnp.broadcast_to(share[None], (angles, *share.shape))
    gradient = lax.all_to_all(spread, "angle", 0, 0, tiled=True).reshape(volume.shape)
    return adam_update(volume, first_moment, second_moment, gradient)


def solution(mesh):
    in_specs = (
        P("tile", None, None, None),
        P("tile", None, None, None),
        P("tile", None, None, None),
        P(),
        P("angle", "tile", None, None, None),
        P("angle", "tile", None),
        P("angle", "tile", None),
        P("angle", None, None),
        P("angle", None, None),
        P("angle", "tile", None),
    )
    out_specs = (
        P("tile", None, None, None),
        P("tile", None, None, None),
        P("tile", None, None, None),
    )
    return jax.shard_map(
        per_device, mesh=mesh, in_specs=in_specs, out_specs=out_specs, check_vma=False
    )
```

time: 471 us -> 223 us (0.47)
  the two profiles are of different devices: /device:TPU:4 before, /device:TPU:74 now
where the time goes in v1:
time: 223 us; the launch traced here: 222 us
  waiting for transfers between devices  96.8 us (43%)
  blocking collectives  55.4 us (25%)
  starting transfers between devices  32 us (14%)
  other arithmetic  14.7 us (7%)
  Pallas kernels  12.3 us (6%)
  local copies, waits for them, and re-layouts  7.6 us (3%)
    all_to_all x1, waiting for transfers between devices, per_device(): lax.all_to_all(returning, 'tile', split_axis=0, concat_axis=0, tiled=True)  46.1 us
    all_to_all x1, waiting for transfers between devices, per_device(): lax.all_to_all(outgoing, 'tile', split_axis=0, concat_axis=0, tiled=True)  43.6 us
    all_to_all x1, blocking collectives, per_device(): lax.all_to_all(spread, 'angle', 0, 0, tiled=True).reshape(volume.shape)  27.7 us
    all_to_all x1, blocking collectives, per_device(): lax.all_to_all(partial_sums.astype(jnp.bfloat16), 'angle', 0, 0, tiled=True)  27.7 us
    pallas_call x1, Pallas kernels, local_gradient(): pl.pallas_call(lambda *refs: wave_kernel(size, chunk, *refs), out_shape=j...  12.3 us
    all_to_all x1, starting transfers between devices, per_device(): lax.all_to_all(returning, 'tile', split_axis=0, concat_axis=0, tiled=True)  11.8 us
    all_to_all x1, starting transfers between devices, per_device(): lax.all_to_all(outgoing, 'tile', split_axis=0, concat_axis=0, tiled=True)  8.05 us
    ppermute x2, starting transfers between devices, from_behind(): return lax.ppermute(array, axis, pairs)  5.75 us
  transfers between devices with their start and end apart: 6, of which 6 were waited for; matrix products, arithmetic and copies ran while one was open for 2% of the time, Pallas kernels for 0%

profile of v1, /device:TPU:74, one launch (start us, length us, event | category | flops | bytes accessed | tf_op | source)
XLA Modules:
  0.0 222.0 jit_solution(1327989943105393705)
XLA Ops:
  0.7 0.7 broadcast_compare_fusion
  1.4 1.6 convert_reduce_fusion.1
  2.9 0.1 fusion.8
  3.1 0.8 select_reduce_fusion
  3.9 0.1 copy.29
  4.0 0.1 copy.32
  4.1 0.1 reshape.242
  4.2 1.1 convert_element_type.55
  5.3 0.7 gather_fusion
  6.0 1.6 broadcast_select_fusion
  7.6 0.0 copy-start.4
  7.6 8.1 %all-to-all-start = ((bf16[32,2,2,32,256]{4,3,2,1,0:T(8,128)(2,1)}), bf16[32,2,2,32,256]{4,3,2,1,0:T(8,128)(2,1)S(1)}, u32[]{:S(2)}, u32[]{:S(2)}) async-start(bf16[32,2,2,32,256]{4,3,2,1,0:T(8,128)(2,1)} %broadcast_select_fusion), calls=%async_computation | async-start | bytes 4194304 | tf_op jit(solution)/shard_map/all_to_all | solution.py:225
  15.6 0.5 broadcast.168
  16.1 0.0 copy-done.4
  16.1 0.7 reduce.3
  16.8 0.1 mul.89
  16.9 0.7 fusion.19
  17.6 0.7 fusion.18
  18.3 0.1 fusion.6
  18.5 43.6 %all-to-all-done = bf16[32,2,2,32,256]{4,3,2,1,0:T(8,128)(2,1)S(1)} async-done(((bf16[32,2,2,32,256]{4,3,2,1,0:T(8,128)(2,1)}), bf16[32,2,2,32,256]{4,3,2,1,0:T(8,128)(2,1)S(1)}, u32[]{:S(2)}, u32[]{:S(2)}) %all-to-all-start) | async-done | bytes 2097184 | tf_op jit(solution)/shard_map/all_to_all | solution.py:225
  62.0 0.6 gather_fusion.1
  62.7 0.3 fusion.22
  62.9 0.2 fusion.5
  63.2 0.1 fusion.24
  63.3 3.5 %collective-permute-start = (bf16[2,2,256,64]{3,2,1,0:T(8,128)(2,1)S(1)}, bf16[2,2,256,64]{3,2,1,0:T(8,128)(2,1)S(1)}, u32[]{:S(2)}, u32[]{:S(2)}) collective-permute-start(bf16[2,2,256,64]{3,2,1,0:T(8,128)(2,1)S(1)} %get-tuple-element.12), channel_id=1, source_target_pairs={{0,1},{1,2},{2,3},{3,4},{4,5},{5,6},{6,7},{7,8},{8,9},{9,10},{10,1... | collective-permute-start | bytes 393224 | tf_op jit(solution)/shard_map/ppermute | solution.py:27
  66.9 2.9 %collective-permute-start.1 = (bf16[2,2,256,64]{3,2,1,0:T(8,128)(2,1)S(1)}, bf16[2,2,256,64]{3,2,1,0:T(8,128)(2,1)S(1)}, u32[]{:S(2)}, u32[]{:S(2)}) collective-permute-start(bf16[2,2,256,64]{3,2,1,0:T(8,128)(2,1)S(1)} %get-tuple-element.13), channel_id=1, source_target_pairs={{1,0},{2,1},{3,2},{4,3},{5,4},{6,5},{7,6},{8,7},{9,8},{10,9},{11,1... | collective-permute-start | bytes 393224 | tf_op jit(solution)/shard_map/ppermute | solution.py:29
  69.8 2.1 collective-permute-done
  71.9 1.8 collective-permute-done.1
  73.7 1.6 maximum_convert_fusion.refs_2_
  75.3 12.3 %waves.1 = f32[4,256,384]{2,1,0:T(8,128)} custom-call(s32[1,8]{1,0:T(1,128)} %bitcast.89, s32[1,8]{1,0:T(1,128)} %bitcast.90, f32[4,256,384]{2,1,0:T(8,128)} %maximum_convert_fusion.refs_2_, f32[2,128,128]{2,1,0:T(8,128)} %refs_3_.1, bf16[8,128,128]{2,1,0:T(8,128)(2,1)} %bitcast.84, bf16[8,256,256]{2,1,0:T(8,128)(2,1)} %constant.15.clone.refs_5_), custom_call_target="tpu_custom_call" | custom-call | tf_op jit(solution)/shard_map/waves/pallas_call | solution.py:157
  87.6 0.0 copy-start
  87.6 1.6 convert_element_type.63
  89.2 0.1 fusion.23
  89.3 2.8 %collective-permute-start.2 = (bf16[2,2,256,64]{3,2,1,0:T(8,128)(2,1)S(1)}, bf16[2,2,256,64]{3,2,1,0:T(8,128)(2,1)S(1)}, u32[]{:S(2)}, u32[]{:S(2)}) collective-permute-start(bf16[2,2,256,64]{3,2,1,0:T(8,128)(2,1)S(1)} %get-tuple-element.10), channel_id=1, source_target_pairs={{0,1},{1,2},{2,3},{3,4},{4,5},{5,6},{6,7},{7,8},{8,9},{9,10},{10,1... | collective-permute-start | bytes 393224 | tf_op jit(solution)/shard_map/ppermute | solution.py:39
  92.2 2.9 %collective-permute-start.3 = (bf16[2,2,256,64]{3,2,1,0:T(8,128)(2,1)S(1)}, bf16[2,2,256,64]{3,2,1,0:T(8,128)(2,1)S(1)}, u32[]{:S(2)}, u32[]{:S(2)}) collective-permute-start(bf16[2,2,256,64]{3,2,1,0:T(8,128)(2,1)S(1)} %get-tuple-element.11), channel_id=1, source_target_pairs={{1,0},{2,1},{3,2},{4,3},{5,4},{6,5},{7,6},{8,7},{9,8},{10,9},{11,1... | collective-permute-start | bytes 393224 | tf_op jit(solution)/shard_map/ppermute | solution.py:39
  95.1 0.1 and_reduce_fusion
  95.2 0.1 copy.30
  95.3 0.1 copy.37
  95.4 0.1 reshape.256
  95.5 0.1 pad.3.clone
  95.6 1.6 collective-permute-done.2
  97.2 1.7 collective-permute-done.3
  99.0 0.0 copy-done
  99.0 0.5 slice_add_fusion
  99.5 0.1 copy.35
  99.6 0.2 fusion
  99.8 0.1 pad_maximum_fusion
  99.9 0.1 copy.36
  100.0 0.7 gather_fusion.2
  100.7 1.6 broadcast_select_fusion.1
  102.3 11.8 %all-to-all-start.1 = ((bf16[32,2,2,32,256]{4,3,2,1,0:T(8,128)(2,1)}), bf16[32,2,2,32,256]{4,3,2,1,0:T(8,128)(2,1)S(1)}, u32[]{:S(2)}, u32[]{:S(2)}) async-start(bf16[32,2,2,32,256]{4,3,2,1,0:T(8,128)(2,1)} %broadcast_select_fusion.1), calls=%async_computation.1 | async-start | bytes 4194304 | tf_op jit(solution)/shard_map/all_to_all | solution.py:265
  114.0 0.1 and.45
  114.2 0.1 copy.28
  114.2 0.1 eq.98
  114.4 46.1 %all-to-all-done.1 = bf16[32,2,2,32,256]{4,3,2,1,0:T(8,128)(2,1)S(1)} async-done(((bf16[32,2,2,32,256]{4,3,2,1,0:T(8,128)(2,1)}), bf16[32,2,2,32,256]{4,3,2,1,0:T(8,128)(2,1)S(1)}, u32[]{:S(2)}, u32[]{:S(2)}) %all-to-all-start.1) | async-done | bytes 2097184 | tf_op jit(solution)/shard_map/all_to_all | solution.py:265
  160.5 2.4 %reshape.237 = bf16[64,16384]{1,0:T(8,128)(2,1)} reshape(bf16[32,2,2,32,256]{4,3,2,1,0:T(8,128)(2,1)S(1)} %all-to-all-done.1) | data formatting | bytes 4194304 | tf_op jit(solution)/shard_map/reshape | solution.py:273
  162.8 2.2 convolution_convert_fusion
  165.0 0.1 convert_element_type.68
  165.2 27.7 %all_to_all.20 = bf16[16,32,256]{2,1,0:T(8,128)(2,1)S(1)} all-to-all(bf16[16,32,256]{2,1,0:T(8,128)(2,1)S(1)} %convert_element_type.68), channel_id=1, replica_groups=mesh['angle'=16,'tile'=32] {'angle'}, dimensions={0} | all-to-all | bytes 524288 | tf_op jit(solution)/shard_map/all_to_all | solution.py:279
  192.9 27.7 %all_to_all.21 = f32[16,32,256]{2,1,0:T(8,128)S(1)} all-to-all(f32[16,32,256]{2,1,0:T(8,128)S(1)} %broadcast_in_dim.81), channel_id=1, replica_groups=mesh['angle'=16,'tile'=32] {'angle'}, dimensions={0} | all-to-all | bytes 1048576 | tf_op jit(solution)/shard_map/all_to_all | solution.py:282
  220.7 0.0 copy-done.1
  220.7 0.0 copy-done.2
  220.7 0.0 copy-done.3
  220.7 1.3 divide_subtract_fusion
  (19 shorter events, 0.3 us)
Async XLA Ops:
  7.6 8.6 %copy-start.4 = (f32[1,1,16]{2,1,0:T(1,128)S(1)}, f32[1,1,16]{2,1,0:T(1,128)}, u32[]{:S(2)}) copy-start(f32[1,1,16]{2,1,0:T(1,128)} %param.20) | copy-start | bytes 196
  7.6 54.5 %all-to-all-start = ((bf16[32,2,2,32,256]{4,3,2,1,0:T(8,128)(2,1)}), bf16[32,2,2,32,256]{4,3,2,1,0:T(8,128)(2,1)S(1)}, u32[]{:S(2)}, u32[]{:S(2)}) async-start(bf16[32,2,2,32,256]{4,3,2,1,0:T(8,128)(2,1)} %broadcast_select_fusion), calls=%async_computation | async-start | bytes 4194304 | tf_op jit(solution)/shard_map/all_to_all | solution.py:225
  63.3 8.6 %collective-permute-start = (bf16[2,2,256,64]{3,2,1,0:T(8,128)(2,1)S(1)}, bf16[2,2,256,64]{3,2,1,0:T(8,128)(2,1)S(1)}, u32[]{:S(2)}, u32[]{:S(2)}) collective-permute-start(bf16[2,2,256,64]{3,2,1,0:T(8,128)(2,1)S(1)} %get-tuple-element.12), channel_id=1, source_target_pairs={{0,1},{1,2},{2,3},{3,4},{4,5},{5,6},{6,7},{7,8},{8,9},{9,10},{10,1... | collective-permute-start | bytes 393224 | tf_op jit(solution)/shard_map/ppermute | solution.py:27
  66.9 6.8 %collective-permute-start.1 = (bf16[2,2,256,64]{3,2,1,0:T(8,128)(2,1)S(1)}, bf16[2,2,256,64]{3,2,1,0:T(8,128)(2,1)S(1)}, u32[]{:S(2)}, u32[]{:S(2)}) collective-permute-start(bf16[2,2,256,64]{3,2,1,0:T(8,128)(2,1)S(1)} %get-tuple-element.13), channel_id=1, source_target_pairs={{1,0},{2,1},{3,2},{4,3},{5,4},{6,5},{7,6},{8,7},{9,8},{10,9},{11,1... | collective-permute-start | bytes 393224 | tf_op jit(solution)/shard_map/ppermute | solution.py:29
  87.6 11.4 %copy-start = (f32[4,256,384]{2,1,0:T(8,128)S(1)}, f32[4,256,384]{2,1,0:T(8,128)}, u32[]{:S(2)}) copy-start(f32[4,256,384]{2,1,0:T(8,128)} %waves.1) | copy-start | bytes 4718596
  89.3 7.9 %collective-permute-start.2 = (bf16[2,2,256,64]{3,2,1,0:T(8,128)(2,1)S(1)}, bf16[2,2,256,64]{3,2,1,0:T(8,128)(2,1)S(1)}, u32[]{:S(2)}, u32[]{:S(2)}) collective-permute-start(bf16[2,2,256,64]{3,2,1,0:T(8,128)(2,1)S(1)} %get-tuple-element.10), channel_id=1, source_target_pairs={{0,1},{1,2},{2,3},{3,4},{4,5},{5,6},{6,7},{7,8},{8,9},{9,10},{10,1... | collective-permute-start | bytes 393224 | tf_op jit(solution)/shard_map/ppermute | solution.py:39
  92.2 6.8 %collective-permute-start.3 = (bf16[2,2,256,64]{3,2,1,0:T(8,128)(2,1)S(1)}, bf16[2,2,256,64]{3,2,1,0:T(8,128)(2,1)S(1)}, u32[]{:S(2)}, u32[]{:S(2)}) collective-permute-start(bf16[2,2,256,64]{3,2,1,0:T(8,128)(2,1)S(1)} %get-tuple-element.11), channel_id=1, source_target_pairs={{1,0},{2,1},{3,2},{4,3},{5,4},{6,5},{7,6},{8,7},{9,8},{10,9},{11,1... | collective-permute-start | bytes 393224 | tf_op jit(solution)/shard_map/ppermute | solution.py:39
  102.3 58.2 %all-to-all-start.1 = ((bf16[32,2,2,32,256]{4,3,2,1,0:T(8,128)(2,1)}), bf16[32,2,2,32,256]{4,3,2,1,0:T(8,128)(2,1)S(1)}, u32[]{:S(2)}, u32[]{:S(2)}) async-start(bf16[32,2,2,32,256]{4,3,2,1,0:T(8,128)(2,1)} %broadcast_select_fusion.1), calls=%async_computation.1 | async-start | bytes 4194304 | tf_op jit(solution)/shard_map/all_to_all | solution.py:265
  162.8 57.9 %copy-start.1 = (f32[8,2,32,256]{3,2,1,0:T(8,128)S(1)}, f32[8,2,32,256]{3,2,1,0:T(8,128)}, u32[]{:S(2)}) copy-start(f32[8,2,32,256]{3,2,1,0:T(8,128)} %param.11) | copy-start | bytes 1572868
  162.8 57.9 %copy-start.2 = (f32[8,2,32,256]{3,2,1,0:T(8,128)S(1)}, f32[8,2,32,256]{3,2,1,0:T(8,128)}, u32[]{:S(2)}) copy-start(f32[8,2,32,256]{3,2,1,0:T(8,128)} %param.12) | copy-start | bytes 1572868
  162.8 57.9 %copy-start.3 = (f32[8,2,32,256]{3,2,1,0:T(8,128)S(1)}, f32[8,2,32,256]{3,2,1,0:T(8,128)}, u32[]{:S(2)}) copy-start(f32[8,2,32,256]{3,2,1,0:T(8,128)} %param.13) | copy-start | bytes 1572868

commit v2 on v1

--- a/solution.py
+++ b/solution.py
@@ -171,6 +171,194 @@
     return out.reshape(layers, parts, high, wide)
 
 
+MESH = pl.DeviceIdType.MESH
+
+
+def place(tile, across):
+    return tile % 2, tile // 2 % across, tile // (2 * across)
+
+
+def greet(axis):
+    count = lax.axis_size(axis)
+    me = lax.axis_index(axis)
+    barrier = pltpu.get_barrier_semaphore()
+
+    def signal(d, carry):
+        pl.semaphore_signal(
+            barrier, inc=1, device_id={axis: lax.rem(me + d, count)}, device_id_type=MESH
+        )
+        return carry
+
+    lax.fori_loop(1, count, signal, 0)
+    pl.semaphore_wait(barrier, count - 1)
+
+
+def direct_copy(d, source, target, send_sem, recv_sem):
+    count = lax.axis_size("tile")
+    me = lax.axis_index("tile")
+    peer = lax.rem(me + d, count)
+    return pltpu.make_async_remote_copy(
+        src_ref=source.at[peer],
+        dst_ref=target.at[me],
+        send_sem=send_sem.at[d],
+        recv_sem=recv_sem.at[d],
+        device_id={"tile": peer},
+        device_id_type=MESH,
+    )
+
+
+def start_direct(source, target, own_sem, send_sem, recv_sem):
+    me = lax.axis_index("tile")
+    own = pltpu.make_async_copy(source.at[me], target.at[me], own_sem)
+    own.start()
+
+    def start(d, carry):
+        direct_copy(d, source, target, send_sem, recv_sem).start()
+        return carry
+
+    lax.fori_loop(1, lax.axis_size("tile"), start, 0)
+    return own
+
+
+def wait_direct(source, target, send_sem, recv_sem):
+    def wait(d, carry):
+        direct_copy(d, source, target, send_sem, recv_sem).wait()
+        return carry
+
+    lax.fori_loop(1, lax.axis_size("tile"), wait, 0)
+
+
+def fetch_kernel(across, rows, direct, extra, got, near, near_sum, run, run_sum, far,
+                 own_sem, send_sem, recv_sem, hop_send, hop_recv):
+    count = lax.axis_size("tile")
+    core, col, row = place(lax.axis_index("tile"), across)
+
+    def hop(k, source, target, tile):
+        return pltpu.make_async_remote_copy(
+            src_ref=source, dst_ref=target, send_sem=hop_send.at[k], recv_sem=hop_recv.at[k],
+            device_id={"tile": tile}, device_id_type=MESH)
+
+    greet("tile")
+    first = hop(0, extra.at[1 - core], near, (row * across + col) * 2 + 1 - core)
+    first.start()
+    first.wait()
+    near_sum[...] = extra[core] + near[...]
+    hops = []
+    for k in range(1, across):
+        to = lax.rem(col + k, across)
+        hops.append(hop(k, near_sum.at[to], run.at[k - 1], (row * across + to) * 2 + core))
+        hops[-1].start()
+    own = start_direct(direct, got, own_sem, send_sem, recv_sem)
+    for copy in hops:
+        copy.wait()
+    total = near_sum[col]
+    for k in range(across - 1):
+        total = total + run[k]
+    run_sum[...] = total
+    hops = []
+    for k in range(1, rows):
+        to = lax.rem(row + k, rows)
+        hops.append(hop(across - 1 + k, run_sum.at[to], far.at[k - 1], (to * across + col) * 2 + core))
+        hops[-1].start()
+    for copy in hops:
+        copy.wait()
+    total = run_sum[row]
+    for k in range(rows - 1):
+        total = total + far[k]
+    got[count] = total
+    own.wait()
+    wait_direct(direct, got, send_sem, recv_sem)
+
+
+def return_kernel(across, rows, direct, extra, got,
+                  own_sem, send_sem, recv_sem, hop_send, hop_recv):
+    count = lax.axis_size("tile")
+    core, col, row = place(lax.axis_index("tile"), across)
+    half = across * rows
+
+    def hop(k, source, target, tile):
+        return pltpu.make_async_remote_copy(
+            src_ref=source, dst_ref=target, send_sem=hop_send.at[k], recv_sem=hop_recv.at[k],
+            device_id={"tile": tile}, device_id_type=MESH)
+
+    greet("tile")
+    base = count + core * half + col * rows
+    mine = pltpu.make_async_copy(extra, got.at[base + row], hop_send.at[across + rows - 1])
+    mine.start()
+    hops = []
+    for k in range(1, rows):
+        to = lax.rem(row + k, rows)
+        hops.append(hop(k, extra, got.at[base + row], (to * across + col) * 2 + core))
+        hops[-1].start()
+    own = start_direct(direct, got, own_sem, send_sem, recv_sem)
+    mine.wait()
+    for copy in hops:
+        copy.wait()
+    hops = []
+    for k in range(1, across):
+        to = lax.rem(col + k, across)
+        part = got.at[pl.ds(base, rows)]
+        hops.append(hop(rows - 1 + k, part, part, (row * across + to) * 2 + core))
+        hops[-1].start()
+    for copy in hops:
+        copy.wait()
+    part = got.at[pl.ds(count + core * half, half)]
+    last = hop(0, part, part, (row * across + col) * 2 + 1 - core)
+    last.start()
+    last.wait()
+    own.wait()
+    wait_direct(direct, got, send_sem, recv_sem)
+
+
+def chips_of(count):
+    across = 4 if count % 8 == 0 else 1
+    return across, count // (2 * across)
+
+
+def by_core(values):
+    across, rows = chips_of(values.shape[0])
+    values = values.reshape(rows, across, 2, *values.shape[1:])
+    return jnp.swapaxes(values, 0, 2)
+
+
+def exchange_sems(count, across, rows):
+    dma = pltpu.SemaphoreType.DMA
+    return [dma, dma((count,)), dma((count,)), dma((across + rows,)), dma((across + rows,))]
+
+
+def fetch(direct, extra):
+    count, high, wide = direct.shape
+    across, rows = chips_of(count)
+    vmem = pl.BlockSpec(memory_space=pltpu.VMEM)
+    buffer = lambda *dims: pltpu.VMEM((*dims, high, wide), direct.dtype)
+    return pl.pallas_call(
+        lambda *refs: fetch_kernel(across, rows, *refs),
+        out_shape=jax.ShapeDtypeStruct((count + 1, high, wide), direct.dtype),
+        in_specs=[vmem, vmem],
+        out_specs=vmem,
+        scratch_shapes=[
+            buffer(across, rows), buffer(across, rows), buffer(across - 1, rows),
+            buffer(rows), buffer(rows - 1), *exchange_sems(count, across, rows)],
+        compiler_params=pltpu.CompilerParams(collective_id=1, has_side_effects=True),
+        name="fetch",
+    )(direct, extra)
+
+
+def give_back(direct, extra):
+    count, high, wide = direct.shape
+    across, rows = chips_of(count)
+    vmem = pl.BlockSpec(memory_space=pltpu.VMEM)
+    return pl.pallas_call(
+        lambda *refs: return_kernel(across, rows, *refs),
+        out_shape=jax.ShapeDtypeStruct((2 * count, high, wide), direct.dtype),
+        in_specs=[vmem, vmem],
+        out_specs=vmem,
+        scratch_shapes=exchange_sems(count, across, rows),
+        compiler_params=pltpu.CompilerParams(collective_id=2, has_side_effects=True),
+        name="give_back",
+    )(direct, extra)
+
+
 def adam_update(params, moment_one, moment_two, gradient):
     fresh_one = BETA_FIRST * moment_one + (1.0 - BETA_FIRST) * gradient
     fresh_two = BETA_SECOND * moment_two + (1.0 - BETA_SECOND) * gradient * gradient
@@ -201,7 +389,7 @@
     row_blocks = interp_weights.shape[2]
     per_slice = slab_width // block_rows
     layers = row_blocks // per_slice
-    capacity = max(2, requests // tile_count)
+    capacity = 2
     group_owner = owner_ids[0]
     group_block = block_ids[0]
     request_slots = jnp.arange(requests, dtype=jnp.int32)
@@ -219,12 +407,14 @@
     blocks = volume.astype(jnp.bfloat16)
     weight = interp_weights[0, 0]
     complement = 1.0 - weight
-    outgoing = jnp.where(
-        send_valid[:, :, None, None, None], blocks[send_block], jnp.zeros((), jnp.bfloat16)
-    )
-    incoming = lax.all_to_all(outgoing, "tile", split_axis=0, concat_axis=0, tiled=True)
+    block_size = (2 * block_rows, slab_width)
+    flat = blocks.reshape(block_count, *block_size)
+    extra_out = jnp.where(
+        by_core(send_valid[:, 1])[..., None, None], flat[by_core(send_block[:, 1])], 0
+    ).astype(jnp.bfloat16)
+    incoming = fetch(flat[send_block[:, 0]], extra_out)
     fetched = (
-        incoming[my_owner, my_rank]
+        incoming[jnp.where(my_rank == 0, my_owner, tile_count)]
         .astype(jnp.float32)
         .reshape(row_blocks, 2, 2, block_rows, slab_width)
     )
@@ -252,27 +442,24 @@
         [weight[:, None, None, None] * grad_rows, complement[:, None, None, None] * grad_rows],
         axis=1,
     )
-    request_grads = request_grads.reshape(requests, 2, block_rows, slab_width).astype(jnp.bfloat16)
+    request_grads = request_grads.reshape(requests, *block_size).astype(jnp.bfloat16)
     owner_range = jnp.arange(tile_count, dtype=jnp.int32)
-    owned_slots = (my_owner[None, None, :] == owner_range[:, None, None]) & (
-        my_rank[None, None, :] == slot_ids[None, :, None]
-    )
-    back_index = jnp.sum(jnp.where(owned_slots, request_slots[None, None, :], 0), axis=2)
-    back_valid = jnp.any(owned_slots, axis=2)
-    returning = jnp.where(
-        back_valid[:, :, None, None, None], request_grads[back_index], jnp.zeros((), jnp.bfloat16)
-    )
-    arrived = lax.all_to_all(returning, "tile", split_axis=0, concat_axis=0, tiled=True)
+    first_of = (my_owner[None, :] == owner_range[:, None]) & (my_rank[None, :] == 0)
+    back_index = jnp.sum(jnp.where(first_of, request_slots[None, :], 0), axis=1)
+    second = jnp.sum(jnp.where(my_rank == 1, request_slots, 0))
+    arrived = give_back(
+        request_grads[back_index],
+        lax.dynamic_index_in_dim(request_grads, second, 0, keepdims=False),
+    )
     selector = (
         send_block[:, :, None] == jnp.arange(block_count, dtype=jnp.int32)[None, None, :]
     ) & send_valid[:, :, None]
-    selector = selector.reshape(tile_count * capacity, block_count).astype(jnp.bfloat16)
+    selector = jnp.concatenate(
+        [selector[:, 0], by_core(selector[:, 1]).reshape(tile_count, block_count)], axis=0
+    ).astype(jnp.bfloat16)
     grad_volume = jnp.einsum(
-        "nb,nx->bx",
-        selector,
-        arrived.reshape(tile_count * capacity, -1),
-        preferred_element_type=jnp.float32,
-    ).reshape(volume.shape)
+        "nb,nhw->bhw", selector, arrived, preferred_element_type=jnp.float32
+    )
     rows_total = block_count * 2 * block_rows
     angles = lax.axis_size("angle")
     partial_sums = grad_volume.reshape(angles, rows_total // angles, slab_width)

time: 223 us -> 190 us (0.85)
  the two profiles are of different devices: /device:TPU:74 before, /device:TPU:14 now
where the time goes in v2:
time: 190 us; the launch traced here: 189 us
  Pallas kernels  93.4 us (49%)
  blocking collectives  50.7 us (27%)
  other arithmetic  13.8 us (7%)
  starting transfers between devices  11.6 us (6%)
  local copies, waits for them, and re-layouts  9.19 us (5%)
  waiting for transfers between devices  4.73 us (2%)
  between operations  2.9 us (2%)
  matrix products  2.81 us (1%)
    pallas_call x1, Pallas kernels, fetch(): pl.pallas_call(lambda *refs: fetch_kernel(across, rows, *refs), out_shape...  42.3 us
    pallas_call x1, Pallas kernels, give_back(): pl.pallas_call(lambda *refs: return_kernel(across, rows, *refs), out_shap...  38.8 us
    all_to_all x1, blocking collectives, per_device(): lax.all_to_all(partial_sums.astype(jnp.bfloat16), 'angle', 0, 0, tiled=True)  28.4 us
    all_to_all x1, blocking collectives, per_device(): lax.all_to_all(spread, 'angle', 0, 0, tiled=True).reshape(volume.shape)  22.2 us
    pallas_call x1, Pallas kernels, local_gradient(): pl.pallas_call(lambda *refs: wave_kernel(size, chunk, *refs), out_shape=j...  12.3 us
    ppermute x2, starting transfers between devices, from_behind(): return lax.ppermute(array, axis, pairs)  6.02 us
  transfers between devices with their start and end apart: 4, of which 3 were waited for; matrix products, arithmetic and copies ran while one was open for 1% of the time, Pallas kernels for 0%

profile of v2, /device:TPU:14, one launch (start us, length us, event | category | flops | bytes accessed | tf_op | source)
XLA Modules:
  0.0 189.1 jit_solution(8642588522869853214)
XLA Ops:
  0.7 0.5 broadcast.135
  1.2 1.3 reduce.11
  2.5 0.1 mul.89
  2.6 0.7 broadcast_compare_fusion
  3.3 0.7 fusion.19
  4.0 1.6 convert_reduce_fusion.1
  5.6 0.1 fusion.10
  5.7 0.8 select_reduce_fusion
  6.6 0.1 select_reduce_fusion.1
  6.7 0.7 fusion.17
  7.4 0.1 reshape_squeeze.18
  7.5 0.1 copy.45
  7.6 0.1 reshape_squeeze.19
  7.7 0.1 copy.46
  7.8 0.1 reshape.165
  8.0 1.1 convert_element_type.57
  9.0 0.6 gather_fusion.1
  9.7 1.6 gather_fusion
  11.3 1.1 broadcast_select_fusion.refs_1_
  12.4 42.3 %fetch.1 = bf16[33,64,256]{2,1,0:T(8,128)(2,1)} custom-call(bf16[32,64,256]{2,1,0:T(8,128)(2,1)} %gather_fusion, bf16[2,4,4,64,256]{4,3,2,1,0:T(8,128)(2,1)} %broadcast_select_fusion.refs_1_), custom_call_target="tpu_custom_call" | custom-call | tf_op jit(solution)/shard_map/fetch/pallas_call | solution.py:334
  54.7 1.9 gather_fusion.2
  56.6 0.3 fusion.22
  56.9 0.2 fusion.8
  57.1 0.1 fusion.24
  57.3 1.9 %collective-permute-start = (bf16[2,2,256,64]{3,2,1,0:T(8,128)(2,1)S(1)}, bf16[2,2,256,64]{3,2,1,0:T(8,128)(2,1)S(1)}, u32[]{:S(2)}, u32[]{:S(2)}) collective-permute-start(bf16[2,2,256,64]{3,2,1,0:T(8,128)(2,1)S(1)} %get-tuple-element.12), channel_id=1, source_target_pairs={{0,1},{1,2},{2,3},{3,4},{4,5},{5,6},{6,7},{7,8},{8,9},{9,10},{10,1... | collective-permute-start | bytes 393224 | tf_op jit(solution)/shard_map/ppermute | solution.py:27
  59.2 3.6 %collective-permute-start.1 = (bf16[2,2,256,64]{3,2,1,0:T(8,128)(2,1)S(1)}, bf16[2,2,256,64]{3,2,1,0:T(8,128)(2,1)S(1)}, u32[]{:S(2)}, u32[]{:S(2)}) collective-permute-start(bf16[2,2,256,64]{3,2,1,0:T(8,128)(2,1)S(1)} %get-tuple-element.13), channel_id=1, source_target_pairs={{1,0},{2,1},{3,2},{4,3},{5,4},{6,5},{7,6},{8,7},{9,8},{10,9},{11,1... | collective-permute-start | bytes 393224 | tf_op jit(solution)/shard_map/ppermute | solution.py:29
  62.9 2.1 %collective-permute-done = bf16[2,2,256,64]{3,2,1,0:T(8,128)(2,1)S(1)} collective-permute-done((bf16[2,2,256,64]{3,2,1,0:T(8,128)(2,1)S(1)}, bf16[2,2,256,64]{3,2,1,0:T(8,128)(2,1)S(1)}, u32[]{:S(2)}, u32[]{:S(2)}) %collective-permute-start) | collective-permute-done | bytes 131104 | tf_op jit(solution)/shard_map/ppermute | solution.py:27
  64.9 1.8 collective-permute-done.1
  66.7 1.6 maximum_convert_fusion.refs_2_
  68.3 12.3 %waves.1 = f32[4,256,384]{2,1,0:T(8,128)} custom-call(s32[1,8]{1,0:T(1,128)} %bitcast.110, s32[1,8]{1,0:T(1,128)} %bitcast.111, f32[4,256,384]{2,1,0:T(8,128)} %maximum_convert_fusion.refs_2_, f32[2,128,128]{2,1,0:T(8,128)} %refs_3_.1, bf16[8,128,128]{2,1,0:T(8,128)(2,1)} %bitcast.102, bf16[8,256,256]{2,1,0:T(8,128)(2,1)} %constant.16.clone.refs_5_), custom_call_target="tpu_custom_call" | custom-call | tf_op jit(solution)/shard_map/waves/pallas_call | solution.py:157
  80.6 0.0 copy-start.4
  80.6 1.5 convert_element_type.65
  82.1 0.0 copy-start
  82.1 0.1 fusion.23
  82.3 4.1 %collective-permute-start.2 = (bf16[2,2,256,64]{3,2,1,0:T(8,128)(2,1)S(1)}, bf16[2,2,256,64]{3,2,1,0:T(8,128)(2,1)S(1)}, u32[]{:S(2)}, u32[]{:S(2)}) collective-permute-start(bf16[2,2,256,64]{3,2,1,0:T(8,128)(2,1)S(1)} %get-tuple-element.10), channel_id=1, source_target_pairs={{0,1},{1,2},{2,3},{3,4},{4,5},{5,6},{6,7},{7,8},{8,9},{9,10},{10,1... | collective-permute-start | bytes 393224 | tf_op jit(solution)/shard_map/ppermute | solution.py:39
  86.4 1.9 %collective-permute-start.3 = (bf16[2,2,256,64]{3,2,1,0:T(8,128)(2,1)S(1)}, bf16[2,2,256,64]{3,2,1,0:T(8,128)(2,1)S(1)}, u32[]{:S(2)}, u32[]{:S(2)}) collective-permute-start(bf16[2,2,256,64]{3,2,1,0:T(8,128)(2,1)S(1)} %get-tuple-element.11), channel_id=1, source_target_pairs={{1,0},{2,1},{3,2},{4,3},{5,4},{6,5},{7,6},{8,7},{9,8},{10,9},{11,1... | collective-permute-start | bytes 393224 | tf_op jit(solution)/shard_map/ppermute | solution.py:39
  88.3 0.0 copy-done.4
  88.3 0.6 fusion.15
  90.3 0.1 copy.42
  90.4 0.1 copy.44
  90.5 0.1 pad.3.clone
  91.2 0.0 collective-permute-done.2
  91.3 0.9 collective-permute-done.3
  92.2 0.0 copy-done
  92.2 0.5 slice_add_fusion
  92.7 0.1 copy.51
  92.8 0.2 multiply_convert_fusion.1
  93.0 0.1 pad_maximum_fusion
  93.1 0.6 dynamic-slice_bitcast_fusion.refs_1_
  93.7 1.6 gather_fusion.3
  95.3 38.8 %give_back.1 = bf16[64,64,256]{2,1,0:T(8,128)(2,1)} custom-call(bf16[32,64,256]{2,1,0:T(8,128)(2,1)} %gather_fusion.3, bf16[64,256]{1,0:T(8,128)(2,1)} %dynamic-slice_bitcast_fusion.refs_1_), custom_call_target="tpu_custom_call" | custom-call | tf_op jit(solution)/shard_map/give_back/pallas_call | solution.py:351
  134.1 2.8 %fusion.2 = bf16[8,64,256]{2,0,1:T(8,128)(2,1)S(1)} fusion(bf16[64,64,256]{2,1,0:T(8,128)(2,1)} %give_back.1, pred[32,8]{0,1:T(8,128)(4,1)S(1)} %copy.44, pred[32,8]{0,1:T(8,128)(4,1)S(1)} %get-tuple-element.14), kind=kOutput, calls=%fused_computation.6 | convolution fusion | flops 16908800 | bytes 2359808 | tf_op jit(solution)/shard_map/nb,nhw->bhw/dot_general | solution.py:460
  136.9 0.0 copy-start.1
  136.9 0.0 copy-start.2
  136.9 0.0 copy-start.3
  137.0 28.4 %all_to_all.10 = bf16[16,32,256]{2,1,0:T(8,128)(2,1)S(1)} all-to-all(bf16[16,32,256]{2,1,0:T(8,128)(2,1)S(1)} %bitcast.101), channel_id=1, replica_groups=mesh['angle'=16,'tile'=32] {'angle'}, dimensions={0} | all-to-all | bytes 524288 | tf_op jit(solution)/shard_map/all_to_all | solution.py:466
  165.5 22.2 %all_to_all.11 = f32[16,32,256]{2,1,0:T(8,128)S(1)} all-to-all(f32[16,32,256]{2,1,0:T(8,128)S(1)} %broadcast_in_dim.81), channel_id=1, replica_groups=mesh['angle'=16,'tile'=32] {'angle'}, dimensions={0} | all-to-all | bytes 1048576 | tf_op jit(solution)/shard_map/all_to_all | solution.py:469
  187.8 0.0 copy-done.1
  187.8 0.0 copy-done.2
  187.8 0.0 copy-done.3
  187.8 1.3 divide_subtract_fusion
  (22 shorter events, 0.4 us)
Async XLA Ops:
  57.3 7.7 %collective-permute-start = (bf16[2,2,256,64]{3,2,1,0:T(8,128)(2,1)S(1)}, bf16[2,2,256,64]{3,2,1,0:T(8,128)(2,1)S(1)}, u32[]{:S(2)}, u32[]{:S(2)}) collective-permute-start(bf16[2,2,256,64]{3,2,1,0:T(8,128)(2,1)S(1)} %get-tuple-element.12), channel_id=1, source_target_pairs={{0,1},{1,2},{2,3},{3,4},{4,5},{5,6},{6,7},{7,8},{8,9},{9,10},{10,1... | collective-permute-start | bytes 393224 | tf_op jit(solution)/shard_map/ppermute | solution.py:27
  59.2 7.5 %collective-permute-start.1 = (bf16[2,2,256,64]{3,2,1,0:T(8,128)(2,1)S(1)}, bf16[2,2,256,64]{3,2,1,0:T(8,128)(2,1)S(1)}, u32[]{:S(2)}, u32[]{:S(2)}) collective-permute-start(bf16[2,2,256,64]{3,2,1,0:T(8,128)(2,1)S(1)} %get-tuple-element.13), channel_id=1, source_target_pairs={{1,0},{2,1},{3,2},{4,3},{5,4},{6,5},{7,6},{8,7},{9,8},{10,9},{11,1... | collective-permute-start | bytes 393224 | tf_op jit(solution)/shard_map/ppermute | solution.py:29
  80.6 7.7 %copy-start.4 = (f32[1,1,16]{2,1,0:T(1,128)S(1)}, f32[1,1,16]{2,1,0:T(1,128)}, u32[]{:S(2)}) copy-start(f32[1,1,16]{2,1,0:T(1,128)} %param.20) | copy-start | bytes 196
  82.1 10.1 %copy-start = (f32[4,256,384]{2,1,0:T(8,128)S(1)}, f32[4,256,384]{2,1,0:T(8,128)}, u32[]{:S(2)}) copy-start(f32[4,256,384]{2,1,0:T(8,128)} %waves.1) | copy-start | bytes 4718596
  82.3 9.0 %collective-permute-start.2 = (bf16[2,2,256,64]{3,2,1,0:T(8,128)(2,1)S(1)}, bf16[2,2,256,64]{3,2,1,0:T(8,128)(2,1)S(1)}, u32[]{:S(2)}, u32[]{:S(2)}) collective-permute-start(bf16[2,2,256,64]{3,2,1,0:T(8,128)(2,1)S(1)} %get-tuple-element.10), channel_id=1, source_target_pairs={{0,1},{1,2},{2,3},{3,4},{4,5},{5,6},{6,7},{7,8},{8,9},{9,10},{10,1... | collective-permute-start | bytes 393224 | tf_op jit(solution)/shard_map/ppermute | solution.py:39
  86.4 5.8 %collective-permute-start.3 = (bf16[2,2,256,64]{3,2,1,0:T(8,128)(2,1)S(1)}, bf16[2,2,256,64]{3,2,1,0:T(8,128)(2,1)S(1)}, u32[]{:S(2)}, u32[]{:S(2)}) collective-permute-start(bf16[2,2,256,64]{3,2,1,0:T(8,128)(2,1)S(1)} %get-tuple-element.11), channel_id=1, source_target_pairs={{1,0},{2,1},{3,2},{4,3},{5,4},{6,5},{7,6},{8,7},{9,8},{10,9},{11,1... | collective-permute-start | bytes 393224 | tf_op jit(solution)/shard_map/ppermute | solution.py:39
  136.9 50.8 %copy-start.1 = (f32[8,2,32,256]{3,2,1,0:T(8,128)S(1)}, f32[8,2,32,256]{3,2,1,0:T(8,128)}, u32[]{:S(2)}) copy-start(f32[8,2,32,256]{3,2,1,0:T(8,128)} %param.11) | copy-start | bytes 1572868
  136.9 50.8 %copy-start.2 = (f32[8,2,32,256]{3,2,1,0:T(8,128)S(1)}, f32[8,2,32,256]{3,2,1,0:T(8,128)}, u32[]{:S(2)}) copy-start(f32[8,2,32,256]{3,2,1,0:T(8,128)} %param.12) | copy-start | bytes 1572868
  136.9 50.8 %copy-start.3 = (f32[8,2,32,256]{3,2,1,0:T(8,128)S(1)}, f32[8,2,32,256]{3,2,1,0:T(8,128)}, u32[]{:S(2)}) copy-start(f32[8,2,32,256]{3,2,1,0:T(8,128)} %param.13) | copy-start | bytes 1572868

commit v3 on v2

--- a/solution.py
+++ b/solution.py
@@ -359,6 +359,111 @@
     )(direct, extra)
 
 
+def angle_kernel(parts, out, landed, partial, other,
+                 in_send, in_recv, pair_send, pair_recv, right_send, right_recv, left_send, left_recv):
+    ring = parts.shape[0]
+    me = lax.axis_index("angle")
+    spot, side = me // 2, me % 2
+
+    def copy(source, target, send_sem, recv_sem, to, at):
+        return pltpu.make_async_remote_copy(
+            src_ref=source, dst_ref=target, send_sem=send_sem, recv_sem=recv_sem,
+            device_id={"angle": to * 2 + at}, device_id_type=MESH)
+
+    barrier = pltpu.get_barrier_semaphore()
+    for k in range(1, ring):
+        pl.semaphore_signal(barrier, inc=1, device_id={"angle": lax.rem(spot + k, ring) * 2 + side},
+                            device_id_type=MESH)
+    pl.semaphore_signal(barrier, inc=1, device_id={"angle": spot * 2 + 1 - side}, device_id_type=MESH)
+    pl.semaphore_wait(barrier, ring)
+
+    copies = []
+    for k in range(1, ring):
+        to = lax.rem(spot + k, ring)
+        copies.append(copy(parts.at[to], landed.at[k - 1], in_send.at[k - 1], in_recv.at[k - 1], to, side))
+        copies[-1].start()
+    for c in copies:
+        c.wait()
+    total = parts[spot].astype(jnp.float32)
+    for k in range(ring - 1):
+        total = total + landed[k].astype(jnp.float32)
+    partial[...] = total
+    pair = copy(partial.at[1 - side], other, pair_send.at[0], pair_recv.at[0], spot, 1 - side)
+    pair.start()
+    pair.wait()
+    out[spot, side] = partial[side] + other[...]
+
+    pair = copy(out.at[spot, side], out.at[spot, side], pair_send.at[1], pair_recv.at[1], spot, 1 - side)
+    pair.start()
+    right, left = lax.rem(spot + 1, ring), lax.rem(spot + ring - 1, ring)
+    far = ring // 2
+    reach = ((far, ring - 1 - far), (ring - 1 - far, far))
+    chunk = (side, 1 - side)
+
+    def to_right(j, step):
+        block = out.at[lax.rem(spot + ring - step, ring), chunk[j]]
+        return copy(block, block, right_send.at[j, step], right_recv.at[j, step], right, side)
+
+    def to_left(j, step):
+        block = out.at[lax.rem(spot + step, ring), chunk[j]]
+        return copy(block, block, left_send.at[j, step], left_recv.at[j, step], left, side)
+
+    def from_left(j, step):
+        block = out.at[lax.rem(spot + ring - step - 1, ring), chunk[j]]
+        return copy(block, block, right_send.at[j, step], right_recv.at[j, step], right, side)
+
+    def from_right(j, step):
+        block = out.at[lax.rem(spot + step + 1, ring), chunk[j]]
+        return copy(block, block, left_send.at[j, step], left_recv.at[j, step], left, side)
+
+    sent = []
+    for j in range(2):
+        if j == 1:
+            pair.wait_send()
+            incoming = out.at[spot, 1 - side]
+            copy(incoming, incoming, pair_send.at[1], pair_recv.at[1], spot, 1 - side).wait_recv()
+        sent += [to_right(j, 0), to_left(j, 0)]
+        sent[-2].start()
+        sent[-1].start()
+    for step in range(far):
+        for j in range(2):
+            if step < reach[j][0]:
+                from_left(j, step).wait_recv()
+                if step + 1 < reach[j][0]:
+                    sent.append(to_right(j, step + 1))
+                    sent[-1].start()
+            if step < reach[j][1]:
+                from_right(j, step).wait_recv()
+                if step + 1 < reach[j][1]:
+                    sent.append(to_left(j, step + 1))
+                    sent[-1].start()
+    for c in sent:
+        c.wait_send()
+
+
+def sum_over_angle(parts):
+    angles, high, wide = parts.shape
+    ring = angles // 2
+    vmem = pl.BlockSpec(memory_space=pltpu.VMEM)
+    dma = pltpu.SemaphoreType.DMA
+    ring_sems = dma((2, ring))
+    out = pl.pallas_call(
+        angle_kernel,
+        out_shape=jax.ShapeDtypeStruct((ring, 2, high, wide), jnp.float32),
+        in_specs=[vmem],
+        out_specs=vmem,
+        scratch_shapes=[
+            pltpu.VMEM((ring - 1, 2, high, wide), parts.dtype),
+            pltpu.VMEM((2, high, wide), jnp.float32),
+            pltpu.VMEM((high, wide), jnp.float32),
+            dma((ring - 1,)), dma((ring - 1,)), dma((2,)), dma((2,)),
+            ring_sems, ring_sems, ring_sems, ring_sems],
+        compiler_params=pltpu.CompilerParams(collective_id=3, has_side_effects=True),
+        name="angle_sum",
+    )(parts.reshape(ring, 2, high, wide))
+    return out.reshape(angles, high, wide)
+
+
 def adam_update(params, moment_one, moment_two, gradient):
     fresh_one = BETA_FIRST * moment_one + (1.0 - BETA_FIRST) * gradient
     fresh_two = BETA_SECOND * moment_two + (1.0 - BETA_SECOND) * gradient * gradient
@@ -389,21 +494,19 @@
     row_blocks = interp_weights.shape[2]
     per_slice = slab_width // block_rows
     layers = row_blocks // per_slice
-    capacity = 2
     group_owner = owner_ids[0]
     group_block = block_ids[0]
     request_slots = jnp.arange(requests, dtype=jnp.int32)
+    my_owner = lax.dynamic_index_in_dim(group_owner, tile_index, 0, keepdims=False)
     earlier = request_slots[None, :] < request_slots[:, None]
-    same_owner = group_owner[:, :, None] == group_owner[:, None, :]
-    group_rank = jnp.sum(same_owner & earlier[None], axis=2)
-    my_owner = lax.dynamic_index_in_dim(group_owner, tile_index, 0, keepdims=False)
-    my_rank = lax.dynamic_index_in_dim(group_rank, tile_index, 0, keepdims=False)
-    slot_ids = jnp.arange(capacity, dtype=jnp.int32)
-    serving = (group_owner == tile_index)[:, None, :] & (
-        group_rank[:, None, :] == slot_ids[None, :, None]
-    )
-    send_block = jnp.sum(jnp.where(serving, group_block[:, None, :], 0), axis=2)
-    send_valid = jnp.any(serving, axis=2)
+    my_rank = jnp.sum((my_owner[:, None] == my_owner[None, :]) & earlier, axis=1)
+    mine = group_owner == tile_index
+    first_slot = jnp.min(jnp.where(mine, request_slots, requests), axis=1)
+    last_slot = jnp.max(jnp.where(mine, request_slots, -1), axis=1)
+    slots = jnp.stack([first_slot, last_slot], axis=1)
+    send_valid = jnp.stack([last_slot >= 0, last_slot > first_slot], axis=1)
+    chosen = slots[:, :, None] == request_slots[None, None, :]
+    send_block = jnp.sum(jnp.where(chosen, group_block[:, None, :], 0), axis=2)
     blocks = volume.astype(jnp.bfloat16)
     weight = interp_weights[0, 0]
     complement = 1.0 - weight
@@ -463,10 +566,7 @@
     rows_total = block_count * 2 * block_rows
     angles = lax.axis_size("angle")
     partial_sums = grad_volume.reshape(angles, rows_total // angles, slab_width)
-    parts = lax.all_to_all(partial_sums.astype(jnp.bfloat16), "angle", 0, 0, tiled=True)
-    share = jnp.sum(parts.astype(jnp.float32), axis=0)
-    spread = jnp.broadcast_to(share[None], (angles, *share.shape))
-    gradient = lax.all_to_all(spread, "angle", 0, 0, tiled=True).reshape(volume.shape)
+    gradient = sum_over_angle(partial_sums.astype(jnp.bfloat16)).reshape(volume.shape)
     return adam_update(volume, first_moment, second_moment, gradient)
 
 

time: 190 us -> 182 us (0.958)
  blocking collectives: 50.7 us -> 0 us
  Pallas kernels: 93.4 us -> 136 us
    all_to_all x2 -> x0, blocking collectives: 50.7 us -> none  [the longest x1 28.4 us: per_device(): lax.all_to_all(partial_sums.astype(jnp.bfloat16), 'angle', 0, 0, tiled=True)]
    pallas_call x0 -> x1, Pallas kernels: none -> 42.9 us  [sum_over_angle(): pl.pallas_call(angle_kernel, out_shape=jax.ShapeDtypeStruct((ring, 2, hig...]
where the time goes in v3:
time: 182 us; the launch traced here: 181 us
  Pallas kernels  136 us (75%)
  other arithmetic  12.8 us (7%)
  starting transfers between devices  11.6 us (6%)
  local copies, waits for them, and re-layouts  9.83 us (5%)
  waiting for transfers between devices  4.72 us (3%)
  between operations  2.94 us (2%)
  matrix products  2.92 us (2%)
    pallas_call x1, Pallas kernels, sum_over_angle(): pl.pallas_call(angle_kernel, out_shape=jax.ShapeDtypeStruct((ring, 2, hig...  42.9 us
    pallas_call x1, Pallas kernels, fetch(): pl.pallas_call(lambda *refs: fetch_kernel(across, rows, *refs), out_shape...  42.3 us
    pallas_call x1, Pallas kernels, give_back(): pl.pallas_call(lambda *refs: return_kernel(across, rows, *refs), out_shap...  38.8 us
    pallas_call x1, Pallas kernels, local_gradient(): pl.pallas_call(lambda *refs: wave_kernel(size, chunk, *refs), out_shape=j...  12.3 us
    ppermute x2, starting transfers between devices, from_behind(): return lax.ppermute(array, axis, pairs)  5.99 us
    ppermute x1, starting transfers between devices, with_halo(): lax.ppermute(head, axis, [((i + 1) % count, i) for i in range(ends)])  3.64 us
  transfers between devices with their start and end apart: 4, of which 3 were waited for; matrix products, arithmetic and copies ran while one was open for 1% of the time, Pallas kernels for 0%

profile of v3, /device:TPU:14, one launch (start us, length us, event | category | flops | bytes accessed | tf_op | source)
XLA Modules:
  0.0 181.1 jit_solution(14814913983911320723)
XLA Ops:
  0.6 0.8 select_reduce_fusion.3
  1.5 0.7 fusion.18
  2.2 0.2 convert_reduce_fusion
  2.4 0.1 select_reduce_fusion.1
  2.5 0.7 fusion.16
  3.2 0.9 select_reduce_fusion
  4.1 0.1 reshape_squeeze.15
  4.2 0.1 copy.50
  4.4 0.1 reshape.167
  4.5 1.1 convert_element_type.54
  5.5 0.1 gt.18
  5.6 0.1 copy.49
  5.8 0.6 gather_fusion.1
  6.4 1.6 gather_fusion
  8.0 1.1 broadcast_select_fusion.refs_1_
  9.2 42.3 %fetch.1 = bf16[33,64,256]{2,1,0:T(8,128)(2,1)} custom-call(bf16[32,64,256]{2,1,0:T(8,128)(2,1)} %gather_fusion, bf16[2,4,4,64,256]{4,3,2,1,0:T(8,128)(2,1)} %broadcast_select_fusion.refs_1_), custom_call_target="tpu_custom_call" | custom-call | tf_op jit(solution)/shard_map/fetch/pallas_call | solution.py:334
  51.5 1.9 %gather_fusion.2 = bf16[32,64,256]{2,1,0:T(8,128)(2,1)S(1)} fusion(bf16[33,64,256]{2,1,0:T(8,128)(2,1)} %fetch.1, s32[1024]{0:T(1024)S(1)} %pad_clamp_fusion.1), kind=kCustom, calls=%fused_computation.2 | custom fusion | bytes 2097280 | tf_op jit(solution)/shard_map/gather | solution.py:520
  53.3 0.0 copy-start.4
  53.3 0.3 fusion.21
  53.6 0.5 broadcast.133
  54.1 0.0 copy-done.4
  54.1 0.7 reduce.7
  54.8 0.1 mul.89
  54.9 0.2 fusion.8
  55.1 0.1 fusion.23
  55.3 1.9 %collective-permute-start = (bf16[2,2,256,64]{3,2,1,0:T(8,128)(2,1)S(1)}, bf16[2,2,256,64]{3,2,1,0:T(8,128)(2,1)S(1)}, u32[]{:S(2)}, u32[]{:S(2)}) collective-permute-start(bf16[2,2,256,64]{3,2,1,0:T(8,128)(2,1)S(1)} %get-tuple-element.14), channel_id=1, source_target_pairs={{0,1},{1,2},{2,3},{3,4},{4,5},{5,6},{6,7},{7,8},{8,9},{9,10},{10,1... | collective-permute-start | bytes 393224 | tf_op jit(solution)/shard_map/ppermute | solution.py:27
  57.2 3.6 %collective-permute-start.1 = (bf16[2,2,256,64]{3,2,1,0:T(8,128)(2,1)S(1)}, bf16[2,2,256,64]{3,2,1,0:T(8,128)(2,1)S(1)}, u32[]{:S(2)}, u32[]{:S(2)}) collective-permute-start(bf16[2,2,256,64]{3,2,1,0:T(8,128)(2,1)S(1)} %get-tuple-element.15), channel_id=1, source_target_pairs={{1,0},{2,1},{3,2},{4,3},{5,4},{6,5},{7,6},{8,7},{9,8},{10,9},{11,1... | collective-permute-start | bytes 393224 | tf_op jit(solution)/shard_map/ppermute | solution.py:29
  60.9 2.0 %collective-permute-done = bf16[2,2,256,64]{3,2,1,0:T(8,128)(2,1)S(1)} collective-permute-done((bf16[2,2,256,64]{3,2,1,0:T(8,128)(2,1)S(1)}, bf16[2,2,256,64]{3,2,1,0:T(8,128)(2,1)S(1)}, u32[]{:S(2)}, u32[]{:S(2)}) %collective-permute-start) | collective-permute-done | bytes 131104 | tf_op jit(solution)/shard_map/ppermute | solution.py:27
  63.0 1.8 collective-permute-done.1
  64.7 1.6 maximum_convert_fusion.refs_2_
  66.3 12.3 %waves.1 = f32[4,256,384]{2,1,0:T(8,128)} custom-call(s32[1,8]{1,0:T(1,128)} %bitcast.109, s32[1,8]{1,0:T(1,128)} %bitcast.110, f32[4,256,384]{2,1,0:T(8,128)} %maximum_convert_fusion.refs_2_, f32[2,128,128]{2,1,0:T(8,128)} %refs_3_.1, bf16[8,128,128]{2,1,0:T(8,128)(2,1)} %bitcast.100, bf16[8,256,256]{2,1,0:T(8,128)(2,1)} %constant.17.clone.refs_5_), custom_call_target="tpu_custom_call" | custom-call | tf_op jit(solution)/shard_map/waves/pallas_call | solution.py:157
  78.6 1.5 convert_element_type.63
  80.1 0.0 copy-start
  80.1 0.1 fusion.22
  80.3 4.1 %collective-permute-start.2 = (bf16[2,2,256,64]{3,2,1,0:T(8,128)(2,1)S(1)}, bf16[2,2,256,64]{3,2,1,0:T(8,128)(2,1)S(1)}, u32[]{:S(2)}, u32[]{:S(2)}) collective-permute-start(bf16[2,2,256,64]{3,2,1,0:T(8,128)(2,1)S(1)} %get-tuple-element.12), channel_id=1, source_target_pairs={{0,1},{1,2},{2,3},{3,4},{4,5},{5,6},{6,7},{7,8},{8,9},{9,10},{10,1... | collective-permute-start | bytes 393224 | tf_op jit(solution)/shard_map/ppermute | solution.py:39
  84.4 1.9 %collective-permute-start.3 = (bf16[2,2,256,64]{3,2,1,0:T(8,128)(2,1)S(1)}, bf16[2,2,256,64]{3,2,1,0:T(8,128)(2,1)S(1)}, u32[]{:S(2)}, u32[]{:S(2)}) collective-permute-start(bf16[2,2,256,64]{3,2,1,0:T(8,128)(2,1)S(1)} %get-tuple-element.13), channel_id=1, source_target_pairs={{1,0},{2,1},{3,2},{4,3},{5,4},{6,5},{7,6},{8,7},{9,8},{10,9},{11,1... | collective-permute-start | bytes 393224 | tf_op jit(solution)/shard_map/ppermute | solution.py:39
  86.3 0.6 fusion.14
  88.2 0.1 copy.46
  88.3 0.1 copy.48
  88.4 0.1 pad.3.clone
  89.2 0.0 collective-permute-done.2
  89.2 0.9 collective-permute-done.3
  90.2 0.0 copy-done
  90.2 0.5 slice_add_fusion
  90.7 0.1 copy.55
  90.8 0.2 multiply_convert_fusion.1
  91.0 0.1 pad_maximum_fusion
  91.1 1.6 gather_fusion.3
  92.7 0.6 dynamic-slice_bitcast_fusion.refs_1_
  93.3 38.8 %give_back.1 = bf16[64,64,256]{2,1,0:T(8,128)(2,1)} custom-call(bf16[32,64,256]{2,1,0:T(8,128)(2,1)} %gather_fusion.3, bf16[64,256]{1,0:T(8,128)(2,1)} %dynamic-slice_bitcast_fusion.refs_1_), custom_call_target="tpu_custom_call" | custom-call | tf_op jit(solution)/shard_map/give_back/pallas_call | solution.py:351
  132.1 0.0 copy-start.1
  132.1 0.0 copy-start.2
  132.1 0.0 copy-start.3
  132.2 2.9 %fusion.2 = bf16[8,64,256]{2,0,1:T(8,128)(2,1)S(1)} fusion(bf16[64,64,256]{2,1,0:T(8,128)(2,1)} %give_back.1, pred[32,8]{0,1:T(8,128)(4,1)S(1)} %copy.48, pred[32,8]{0,1:T(8,128)(4,1)S(1)} %get-tuple-element.16), kind=kOutput, calls=%fused_computation.6 | convolution fusion | flops 16908800 | bytes 2359808 | tf_op jit(solution)/shard_map/nb,nhw->bhw/dot_general | solution.py:563
  135.1 0.8 copy.57
  135.8 42.9 %angle_sum.1 = f32[8,2,32,256]{3,2,1,0:T(8,128)} custom-call(bf16[8,2,32,256]{3,2,1,0:T(8,128)(2,1)} %bitcast.99), custom_call_target="tpu_custom_call" | custom-call | tf_op jit(solution)/shard_map/angle_sum/pallas_call | solution.py:450
  178.7 0.0 copy-done.1
  178.7 0.0 copy-done.2
  178.7 0.0 copy-done.3
  178.7 2.4 %divide_subtract_fusion = (f32[8,2,32,256]{3,2,1,0:T(8,128)}, f32[8,2,32,256]{3,2,1,0:T(8,128)}, f32[8,2,32,256]{3,2,1,0:T(8,128)}) fusion(f32[8,2,32,256]{3,2,1,0:T(8,128)S(1)} %copy-done.1, f32[8,2,32,256]{3,2,1,0:T(8,128)} %angle_sum.1, f32[8,2,32,256]{3,2,1,0:T(8,128)S(1)} %copy-done.2, f32[8,2,32,256]{3,2,1,0:T(8,128)S(1)} %copy-done.3), kind=kLoop, calls=%fused_computation.20 | loop fusion | flops 1441792 | bytes 3670016 | tf_op jit(solution)/shard_map/sub | solution.py:470
  (21 shorter events, 0.3 us)
Async XLA Ops:
  53.3 0.8 copy-start.4
  55.3 7.7 %collective-permute-start = (bf16[2,2,256,64]{3,2,1,0:T(8,128)(2,1)S(1)}, bf16[2,2,256,64]{3,2,1,0:T(8,128)(2,1)S(1)}, u32[]{:S(2)}, u32[]{:S(2)}) collective-permute-start(bf16[2,2,256,64]{3,2,1,0:T(8,128)(2,1)S(1)} %get-tuple-element.14), channel_id=1, source_target_pairs={{0,1},{1,2},{2,3},{3,4},{4,5},{5,6},{6,7},{7,8},{8,9},{9,10},{10,1... | collective-permute-start | bytes 393224 | tf_op jit(solution)/shard_map/ppermute | solution.py:27
  57.2 7.5 %collective-permute-start.1 = (bf16[2,2,256,64]{3,2,1,0:T(8,128)(2,1)S(1)}, bf16[2,2,256,64]{3,2,1,0:T(8,128)(2,1)S(1)}, u32[]{:S(2)}, u32[]{:S(2)}) collective-permute-start(bf16[2,2,256,64]{3,2,1,0:T(8,128)(2,1)S(1)} %get-tuple-element.15), channel_id=1, source_target_pairs={{1,0},{2,1},{3,2},{4,3},{5,4},{6,5},{7,6},{8,7},{9,8},{10,9},{11,1... | collective-permute-start | bytes 393224 | tf_op jit(solution)/shard_map/ppermute | solution.py:29
  80.1 10.1 %copy-start = (f32[4,256,384]{2,1,0:T(8,128)S(1)}, f32[4,256,384]{2,1,0:T(8,128)}, u32[]{:S(2)}) copy-start(f32[4,256,384]{2,1,0:T(8,128)} %waves.1) | copy-start | bytes 4718596
  80.3 8.9 %collective-permute-start.2 = (bf16[2,2,256,64]{3,2,1,0:T(8,128)(2,1)S(1)}, bf16[2,2,256,64]{3,2,1,0:T(8,128)(2,1)S(1)}, u32[]{:S(2)}, u32[]{:S(2)}) collective-permute-start(bf16[2,2,256,64]{3,2,1,0:T(8,128)(2,1)S(1)} %get-tuple-element.12), channel_id=1, source_target_pairs={{0,1},{1,2},{2,3},{3,4},{4,5},{5,6},{6,7},{7,8},{8,9},{9,10},{10,1... | collective-permute-start | bytes 393224 | tf_op jit(solution)/shard_map/ppermute | solution.py:39
  84.4 5.8 %collective-permute-start.3 = (bf16[2,2,256,64]{3,2,1,0:T(8,128)(2,1)S(1)}, bf16[2,2,256,64]{3,2,1,0:T(8,128)(2,1)S(1)}, u32[]{:S(2)}, u32[]{:S(2)}) collective-permute-start(bf16[2,2,256,64]{3,2,1,0:T(8,128)(2,1)S(1)} %get-tuple-element.13), channel_id=1, source_target_pairs={{1,0},{2,1},{3,2},{4,3},{5,4},{6,5},{7,6},{8,7},{9,8},{10,9},{11,1... | collective-permute-start | bytes 393224 | tf_op jit(solution)/shard_map/ppermute | solution.py:39
  132.1 46.6 %copy-start.1 = (f32[8,2,32,256]{3,2,1,0:T(8,128)S(1)}, f32[8,2,32,256]{3,2,1,0:T(8,128)}, u32[]{:S(2)}) copy-start(f32[8,2,32,256]{3,2,1,0:T(8,128)} %param.11) | copy-start | bytes 1572868
  132.1 46.6 %copy-start.2 = (f32[8,2,32,256]{3,2,1,0:T(8,128)S(1)}, f32[8,2,32,256]{3,2,1,0:T(8,128)}, u32[]{:S(2)}) copy-start(f32[8,2,32,256]{3,2,1,0:T(8,128)} %param.12) | copy-start | bytes 1572868
  132.1 46.6 %copy-start.3 = (f32[8,2,32,256]{3,2,1,0:T(8,128)S(1)}, f32[8,2,32,256]{3,2,1,0:T(8,128)}, u32[]{:S(2)}) copy-start(f32[8,2,32,256]{3,2,1,0:T(8,128)} %param.13) | copy-start | bytes 1572868

commit v4 on v3

--- a/solution.py
+++ b/solution.py
@@ -207,16 +207,18 @@
     )
 
 
-def start_direct(source, target, own_sem, send_sem, recv_sem):
+def start_direct(first, last, source, target, send_sem, recv_sem):
+    def start(d, carry):
+        direct_copy(d, source, target, send_sem, recv_sem).start()
+        return carry
+
+    lax.fori_loop(first, last, start, 0)
+
+
+def keep_own(source, target, own_sem):
     me = lax.axis_index("tile")
     own = pltpu.make_async_copy(source.at[me], target.at[me], own_sem)
     own.start()
-
-    def start(d, carry):
-        direct_copy(d, source, target, send_sem, recv_sem).start()
-        return carry
-
-    lax.fori_loop(1, lax.axis_size("tile"), start, 0)
     return own
 
 
@@ -241,6 +243,8 @@
     greet("tile")
     first = hop(0, extra.at[1 - core], near, (row * across + col) * 2 + 1 - core)
     first.start()
+    start_direct(1, count // 2, direct, got, send_sem, recv_sem)
+    own = keep_own(direct, got, own_sem)
     first.wait()
     near_sum[...] = extra[core] + near[...]
     hops = []
@@ -248,7 +252,7 @@
         to = lax.rem(col + k, across)
         hops.append(hop(k, near_sum.at[to], run.at[k - 1], (row * across + to) * 2 + core))
         hops[-1].start()
-    own = start_direct(direct, got, own_sem, send_sem, recv_sem)
+    start_direct(count // 2, count, direct, got, send_sem, recv_sem)
     for copy in hops:
         copy.wait()
     total = near_sum[col]
@@ -290,7 +294,8 @@
         to = lax.rem(row + k, rows)
         hops.append(hop(k, extra, got.at[base + row], (to * across + col) * 2 + core))
         hops[-1].start()
-    own = start_direct(direct, got, own_sem, send_sem, recv_sem)
+    start_direct(1, count // 2, direct, got, send_sem, recv_sem)
+    own = keep_own(direct, got, own_sem)
     mine.wait()
     for copy in hops:
         copy.wait()
@@ -300,6 +305,7 @@
         part = got.at[pl.ds(base, rows)]
         hops.append(hop(rows - 1 + k, part, part, (row * across + to) * 2 + core))
         hops[-1].start()
+    start_direct(count // 2, count, direct, got, send_sem, recv_sem)
     for copy in hops:
         copy.wait()
     part = got.at[pl.ds(count + core * half, half)]
@@ -388,40 +394,32 @@
     for k in range(ring - 1):
         total = total + landed[k].astype(jnp.float32)
     partial[...] = total
-    pair = copy(partial.at[1 - side], other, pair_send.at[0], pair_recv.at[0], spot, 1 - side)
+    pair = copy(partial, other, pair_send, pair_recv, spot, 1 - side)
     pair.start()
     pair.wait()
-    out[spot, side] = partial[side] + other[...]
-
-    pair = copy(out.at[spot, side], out.at[spot, side], pair_send.at[1], pair_recv.at[1], spot, 1 - side)
-    pair.start()
+    out[spot] = partial[...] + other[...]
     right, left = lax.rem(spot + 1, ring), lax.rem(spot + ring - 1, ring)
     far = ring // 2
     reach = ((far, ring - 1 - far), (ring - 1 - far, far))
-    chunk = (side, 1 - side)
 
     def to_right(j, step):
-        block = out.at[lax.rem(spot + ring - step, ring), chunk[j]]
+        block = out.at[lax.rem(spot + ring - step, ring), j]
         return copy(block, block, right_send.at[j, step], right_recv.at[j, step], right, side)
 
     def to_left(j, step):
-        block = out.at[lax.rem(spot + step, ring), chunk[j]]
+        block = out.at[lax.rem(spot + step, ring), j]
         return copy(block, block, left_send.at[j, step], left_recv.at[j, step], left, side)
 
     def from_left(j, step):
-        block = out.at[lax.rem(spot + ring - step - 1, ring), chunk[j]]
+        block = out.at[lax.rem(spot + ring - step - 1, ring), j]
         return copy(block, block, right_send.at[j, step], right_recv.at[j, step], right, side)
 
     def from_right(j, step):
-        block = out.at[lax.rem(spot + step + 1, ring), chunk[j]]
+        block = out.at[lax.rem(spot + step + 1, ring), j]
         return copy(block, block, left_send.at[j, step], left_recv.at[j, step], left, side)
 
     sent = []
     for j in range(2):
-        if j == 1:
-            pair.wait_send()
-            incoming = out.at[spot, 1 - side]
-            copy(incoming, incoming, pair_send.at[1], pair_recv.at[1], spot, 1 - side).wait_recv()
         sent += [to_right(j, 0), to_left(j, 0)]
         sent[-2].start()
         sent[-1].start()
@@ -455,8 +453,8 @@
         scratch_shapes=[
             pltpu.VMEM((ring - 1, 2, high, wide), parts.dtype),
             pltpu.VMEM((2, high, wide), jnp.float32),
-            pltpu.VMEM((high, wide), jnp.float32),
-            dma((ring - 1,)), dma((ring - 1,)), dma((2,)), dma((2,)),
+            pltpu.VMEM((2, high, wide), jnp.float32),
+            dma((ring - 1,)), dma((ring - 1,)), dma, dma,
             ring_sems, ring_sems, ring_sems, ring_sems],
         compiler_params=pltpu.CompilerParams(collective_id=3, has_side_effects=True),
         name="angle_sum",

time: 182 us -> 177 us (0.973)
  Pallas kernels: 136 us -> 132 us
    pallas_call x1, Pallas kernels: 42.3 us -> 38.9 us  [fetch(): pl.pallas_call(lambda *refs: fetch_kernel(across, rows, *refs), out_shape...]
    pallas_call x1, Pallas kernels: 42.9 us -> 40.8 us  [sum_over_angle(): pl.pallas_call(angle_kernel, out_shape=jax.ShapeDtypeStruct((ring, 2, hig...]
where the time goes in v4:
time: 177 us
  Pallas kernels  132 us (75%)
  other arithmetic  12.8 us (7%)
  starting transfers between devices  11.4 us (6%)
  local copies, waits for them, and re-layouts  9.83 us (6%)
  waiting for transfers between devices  4.72 us (3%)
  between operations  2.94 us (2%)
  matrix products  2.92 us (2%)
    pallas_call x1, Pallas kernels, sum_over_angle(): pl.pallas_call(angle_kernel, out_shape=jax.ShapeDtypeStruct((ring, 2, hig...  40.8 us
    pallas_call x1, Pallas kernels, give_back(): pl.pallas_call(lambda *refs: return_kernel(across, rows, *refs), out_shap...  40.1 us
    pallas_call x1, Pallas kernels, fetch(): pl.pallas_call(lambda *refs: fetch_kernel(across, rows, *refs), out_shape...  38.9 us
    pallas_call x1, Pallas kernels, local_gradient(): pl.pallas_call(lambda *refs: wave_kernel(size, chunk, *refs), out_shape=j...  12.3 us
    ppermute x2, starting transfers between devices, from_behind(): return lax.ppermute(array, axis, pairs)  5.86 us
    ppermute x1, starting transfers between devices, with_halo(): lax.ppermute(head, axis, [((i + 1) % count, i) for i in range(ends)])  3.64 us
  transfers between devices with their start and end apart: 4, of which 3 were waited for; matrix products, arithmetic and copies ran while one was open for 1% of the time, Pallas kernels for 0%

profile of v4, /device:TPU:14, one launch (start us, length us, event | category | flops | bytes accessed | tf_op | source)
XLA Modules:
  0.0 176.7 jit_solution(12842075731635516502)
XLA Ops:
  0.6 0.8 select_reduce_fusion.3
  1.5 0.7 fusion.18
  2.2 0.2 convert_reduce_fusion
  2.4 0.1 select_reduce_fusion.1
  2.5 0.7 fusion.16
  3.2 0.9 select_reduce_fusion
  4.1 0.1 reshape_squeeze.15
  4.2 0.1 copy.50
  4.4 0.1 reshape.167
  4.5 1.1 convert_element_type.54
  5.5 0.1 gt.18
  5.6 0.1 copy.49
  5.8 0.6 gather_fusion.1
  6.4 1.6 gather_fusion
  8.0 1.1 broadcast_select_fusion.refs_1_
  9.2 38.9 %fetch.1 = bf16[33,64,256]{2,1,0:T(8,128)(2,1)} custom-call(bf16[32,64,256]{2,1,0:T(8,128)(2,1)} %gather_fusion, bf16[2,4,4,64,256]{4,3,2,1,0:T(8,128)(2,1)} %broadcast_select_fusion.refs_1_), custom_call_target="tpu_custom_call" | custom-call | tf_op jit(solution)/shard_map/fetch/pallas_call | solution.py:340
  48.0 1.9 %gather_fusion.2 = bf16[32,64,256]{2,1,0:T(8,128)(2,1)S(1)} fusion(bf16[33,64,256]{2,1,0:T(8,128)(2,1)} %fetch.1, s32[1024]{0:T(1024)S(1)} %pad_clamp_fusion.1), kind=kCustom, calls=%fused_computation.2 | custom fusion | bytes 2097280 | tf_op jit(solution)/shard_map/gather | solution.py:518
  49.9 0.0 copy-start.4
  49.9 0.3 fusion.21
  50.2 0.5 broadcast.133
  50.7 0.0 copy-done.4
  50.7 0.7 reduce.7
  51.4 0.1 mul.89
  51.5 0.2 fusion.8
  51.7 0.1 fusion.23
  51.8 1.9 %collective-permute-start = (bf16[2,2,256,64]{3,2,1,0:T(8,128)(2,1)S(1)}, bf16[2,2,256,64]{3,2,1,0:T(8,128)(2,1)S(1)}, u32[]{:S(2)}, u32[]{:S(2)}) collective-permute-start(bf16[2,2,256,64]{3,2,1,0:T(8,128)(2,1)S(1)} %get-tuple-element.14), channel_id=1, source_target_pairs={{0,1},{1,2},{2,3},{3,4},{4,5},{5,6},{6,7},{7,8},{8,9},{9,10},{10,1... | collective-permute-start | bytes 393224 | tf_op jit(solution)/shard_map/ppermute | solution.py:27
  53.8 3.6 %collective-permute-start.1 = (bf16[2,2,256,64]{3,2,1,0:T(8,128)(2,1)S(1)}, bf16[2,2,256,64]{3,2,1,0:T(8,128)(2,1)S(1)}, u32[]{:S(2)}, u32[]{:S(2)}) collective-permute-start(bf16[2,2,256,64]{3,2,1,0:T(8,128)(2,1)S(1)} %get-tuple-element.15), channel_id=1, source_target_pairs={{1,0},{2,1},{3,2},{4,3},{5,4},{6,5},{7,6},{8,7},{9,8},{10,9},{11,1... | collective-permute-start | bytes 393224 | tf_op jit(solution)/shard_map/ppermute | solution.py:29
  57.5 2.0 %collective-permute-done = bf16[2,2,256,64]{3,2,1,0:T(8,128)(2,1)S(1)} collective-permute-done((bf16[2,2,256,64]{3,2,1,0:T(8,128)(2,1)S(1)}, bf16[2,2,256,64]{3,2,1,0:T(8,128)(2,1)S(1)}, u32[]{:S(2)}, u32[]{:S(2)}) %collective-permute-start) | collective-permute-done | bytes 131104 | tf_op jit(solution)/shard_map/ppermute | solution.py:27
  59.5 1.8 collective-permute-done.1
  61.3 1.6 maximum_convert_fusion.refs_2_
  62.9 12.3 %waves.1 = f32[4,256,384]{2,1,0:T(8,128)} custom-call(s32[1,8]{1,0:T(1,128)} %bitcast.109, s32[1,8]{1,0:T(1,128)} %bitcast.110, f32[4,256,384]{2,1,0:T(8,128)} %maximum_convert_fusion.refs_2_, f32[2,128,128]{2,1,0:T(8,128)} %refs_3_.1, bf16[8,128,128]{2,1,0:T(8,128)(2,1)} %bitcast.100, bf16[8,256,256]{2,1,0:T(8,128)(2,1)} %constant.17.clone.refs_5_), custom_call_target="tpu_custom_call" | custom-call | tf_op jit(solution)/shard_map/waves/pallas_call | solution.py:157
  75.2 1.5 convert_element_type.63
  76.7 0.0 copy-start
  76.7 0.1 fusion.22
  76.8 3.6 %collective-permute-start.2 = (bf16[2,2,256,64]{3,2,1,0:T(8,128)(2,1)S(1)}, bf16[2,2,256,64]{3,2,1,0:T(8,128)(2,1)S(1)}, u32[]{:S(2)}, u32[]{:S(2)}) collective-permute-start(bf16[2,2,256,64]{3,2,1,0:T(8,128)(2,1)S(1)} %get-tuple-element.12), channel_id=1, source_target_pairs={{0,1},{1,2},{2,3},{3,4},{4,5},{5,6},{6,7},{7,8},{8,9},{9,10},{10,1... | collective-permute-start | bytes 393224 | tf_op jit(solution)/shard_map/ppermute | solution.py:39
  80.4 2.3 %collective-permute-start.3 = (bf16[2,2,256,64]{3,2,1,0:T(8,128)(2,1)S(1)}, bf16[2,2,256,64]{3,2,1,0:T(8,128)(2,1)S(1)}, u32[]{:S(2)}, u32[]{:S(2)}) collective-permute-start(bf16[2,2,256,64]{3,2,1,0:T(8,128)(2,1)S(1)} %get-tuple-element.13), channel_id=1, source_target_pairs={{1,0},{2,1},{3,2},{4,3},{5,4},{6,5},{7,6},{8,7},{9,8},{10,9},{11,1... | collective-permute-start | bytes 393224 | tf_op jit(solution)/shard_map/ppermute | solution.py:39
  82.7 0.6 fusion.14
  84.6 0.1 copy.46
  84.8 0.1 copy.48
  84.8 0.1 pad.3.clone
  85.6 0.0 collective-permute-done.2
  85.7 0.9 collective-permute-done.3
  86.6 0.0 copy-done
  86.6 0.5 slice_add_fusion
  87.1 0.1 copy.55
  87.2 0.2 multiply_convert_fusion.1
  87.4 0.1 pad_maximum_fusion
  87.5 1.6 gather_fusion.3
  89.1 0.6 dynamic-slice_bitcast_fusion.refs_1_
  89.7 40.1 %give_back.1 = bf16[64,64,256]{2,1,0:T(8,128)(2,1)} custom-call(bf16[32,64,256]{2,1,0:T(8,128)(2,1)} %gather_fusion.3, bf16[64,256]{1,0:T(8,128)(2,1)} %dynamic-slice_bitcast_fusion.refs_1_), custom_call_target="tpu_custom_call" | custom-call | tf_op jit(solution)/shard_map/give_back/pallas_call | solution.py:357
  129.8 0.0 copy-start.1
  129.9 0.0 copy-start.2
  129.9 0.0 copy-start.3
  129.9 2.9 %fusion.2 = bf16[8,64,256]{2,0,1:T(8,128)(2,1)S(1)} fusion(bf16[64,64,256]{2,1,0:T(8,128)(2,1)} %give_back.1, pred[32,8]{0,1:T(8,128)(4,1)S(1)} %copy.48, pred[32,8]{0,1:T(8,128)(4,1)S(1)} %get-tuple-element.16), kind=kOutput, calls=%fused_computation.6 | convolution fusion | flops 16908800 | bytes 2359808 | tf_op jit(solution)/shard_map/nb,nhw->bhw/dot_general | solution.py:561
  132.8 0.8 copy.57
  133.6 40.8 %angle_sum.1 = f32[8,2,32,256]{3,2,1,0:T(8,128)} custom-call(bf16[8,2,32,256]{3,2,1,0:T(8,128)(2,1)} %bitcast.99), custom_call_target="tpu_custom_call" | custom-call | tf_op jit(solution)/shard_map/angle_sum/pallas_call | solution.py:448
  174.3 0.0 copy-done.1
  174.3 0.0 copy-done.2
  174.4 0.0 copy-done.3
  174.4 2.4 %divide_subtract_fusion = (f32[8,2,32,256]{3,2,1,0:T(8,128)}, f32[8,2,32,256]{3,2,1,0:T(8,128)}, f32[8,2,32,256]{3,2,1,0:T(8,128)}) fusion(f32[8,2,32,256]{3,2,1,0:T(8,128)S(1)} %copy-done.1, f32[8,2,32,256]{3,2,1,0:T(8,128)} %angle_sum.1, f32[8,2,32,256]{3,2,1,0:T(8,128)S(1)} %copy-done.2, f32[8,2,32,256]{3,2,1,0:T(8,128)S(1)} %copy-done.3), kind=kLoop, calls=%fused_computation.20 | loop fusion | flops 1441792 | bytes 3670016 | tf_op jit(solution)/shard_map/sub | solution.py:468
  (21 shorter events, 0.3 us)
Async XLA Ops:
  49.9 0.8 copy-start.4
  51.8 7.7 %collective-permute-start = (bf16[2,2,256,64]{3,2,1,0:T(8,128)(2,1)S(1)}, bf16[2,2,256,64]{3,2,1,0:T(8,128)(2,1)S(1)}, u32[]{:S(2)}, u32[]{:S(2)}) collective-permute-start(bf16[2,2,256,64]{3,2,1,0:T(8,128)(2,1)S(1)} %get-tuple-element.14), channel_id=1, source_target_pairs={{0,1},{1,2},{2,3},{3,4},{4,5},{5,6},{6,7},{7,8},{8,9},{9,10},{10,1... | collective-permute-start | bytes 393224 | tf_op jit(solution)/shard_map/ppermute | solution.py:27
  53.8 7.5 %collective-permute-start.1 = (bf16[2,2,256,64]{3,2,1,0:T(8,128)(2,1)S(1)}, bf16[2,2,256,64]{3,2,1,0:T(8,128)(2,1)S(1)}, u32[]{:S(2)}, u32[]{:S(2)}) collective-permute-start(bf16[2,2,256,64]{3,2,1,0:T(8,128)(2,1)S(1)} %get-tuple-element.15), channel_id=1, source_target_pairs={{1,0},{2,1},{3,2},{4,3},{5,4},{6,5},{7,6},{8,7},{9,8},{10,9},{11,1... | collective-permute-start | bytes 393224 | tf_op jit(solution)/shard_map/ppermute | solution.py:29
  76.7 9.9 %copy-start = (f32[4,256,384]{2,1,0:T(8,128)S(1)}, f32[4,256,384]{2,1,0:T(8,128)}, u32[]{:S(2)}) copy-start(f32[4,256,384]{2,1,0:T(8,128)} %waves.1) | copy-start | bytes 4718596
  76.8 8.8 %collective-permute-start.2 = (bf16[2,2,256,64]{3,2,1,0:T(8,128)(2,1)S(1)}, bf16[2,2,256,64]{3,2,1,0:T(8,128)(2,1)S(1)}, u32[]{:S(2)}, u32[]{:S(2)}) collective-permute-start(bf16[2,2,256,64]{3,2,1,0:T(8,128)(2,1)S(1)} %get-tuple-element.12), channel_id=1, source_target_pairs={{0,1},{1,2},{2,3},{3,4},{4,5},{5,6},{6,7},{7,8},{8,9},{9,10},{10,1... | collective-permute-start | bytes 393224 | tf_op jit(solution)/shard_map/ppermute | solution.py:39
  80.4 6.2 %collective-permute-start.3 = (bf16[2,2,256,64]{3,2,1,0:T(8,128)(2,1)S(1)}, bf16[2,2,256,64]{3,2,1,0:T(8,128)(2,1)S(1)}, u32[]{:S(2)}, u32[]{:S(2)}) collective-permute-start(bf16[2,2,256,64]{3,2,1,0:T(8,128)(2,1)S(1)} %get-tuple-element.13), channel_id=1, source_target_pairs={{1,0},{2,1},{3,2},{4,3},{5,4},{6,5},{7,6},{8,7},{9,8},{10,9},{11,1... | collective-permute-start | bytes 393224 | tf_op jit(solution)/shard_map/ppermute | solution.py:39
  129.8 44.5 %copy-start.1 = (f32[8,2,32,256]{3,2,1,0:T(8,128)S(1)}, f32[8,2,32,256]{3,2,1,0:T(8,128)}, u32[]{:S(2)}) copy-start(f32[8,2,32,256]{3,2,1,0:T(8,128)} %param.11) | copy-start | bytes 1572868
  129.9 44.5 %copy-start.2 = (f32[8,2,32,256]{3,2,1,0:T(8,128)S(1)}, f32[8,2,32,256]{3,2,1,0:T(8,128)}, u32[]{:S(2)}) copy-start(f32[8,2,32,256]{3,2,1,0:T(8,128)} %param.12) | copy-start | bytes 1572868
  129.9 44.5 %copy-start.3 = (f32[8,2,32,256]{3,2,1,0:T(8,128)S(1)}, f32[8,2,32,256]{3,2,1,0:T(8,128)}, u32[]{:S(2)}) copy-start(f32[8,2,32,256]{3,2,1,0:T(8,128)} %param.13) | copy-start | bytes 1572868

commit v5 on v4

--- a/solution.py
+++ b/solution.py
@@ -14,23 +14,6 @@
 BETA_SECOND = 0.999
 STEP_SIZE = 0.05
 EPSILON = 1e-08
-
-
-def with_halo(cells, sides, width):
-    for axis, dim in sides:
-        count = lax.axis_size(axis)
-        ends = count - 1
-        head = lax.slice_in_dim(cells, 0, width, axis=dim)
-        tail = lax.slice_in_dim(cells, cells.shape[dim] - width, cells.shape[dim], axis=dim)
-        cells = jnp.concatenate(
-            [
-                lax.ppermute(tail, axis, [(i, (i + 1) % count) for i in range(ends)]),
-                cells,
-                lax.ppermute(head, axis, [((i + 1) % count, i) for i in range(ends)]),
-            ],
-            axis=dim,
-        )
-    return cells
 
 
 def from_behind(array, axis, by):
@@ -69,7 +52,8 @@
     return jnp.dot(a, b, preferred_element_type=jnp.float32)
 
 
-def wave_kernel(size, chunk, rows_ref, cols_ref, obj_ref, probe_ref, amp_ref, tab_ref, acc_ref):
+def wave_kernel(size, chunk, rows_ref, cols_ref, tile_ref, before_ref, after_ref,
+                probe_ref, amp_ref, tab_ref, mid_ref, left_ref, right_ref, obj_ref, acc_ref):
     probes = amp_ref.shape[0]
     n = size
 
@@ -90,6 +74,11 @@
             out_imag += [full[n:, :n], full[n:, n:]]
         return out_real, out_imag
 
+    margin = before_ref.shape[2]
+    inner = tile_ref.shape[2]
+    for c in range(4):
+        obj_ref[c] = jnp.concatenate(
+            [ref[c].astype(jnp.float32) for ref in (before_ref, tile_ref, after_ref)], 1)
     acc_ref[...] = jnp.zeros_like(acc_ref)
     p_real = probe_ref[0]
     p_imag = probe_ref[1]
@@ -144,31 +133,32 @@
         return carry
 
     lax.fori_loop(0, probes // chunk, body, 0)
-
-
-def local_gradient(padded, probe, rows_list, cols_list, amplitudes):
-    layers, parts, high, wide = padded.shape
+    for c in range(4):
+        total = acc_ref[c]
+        mid_ref[c] = total[:, margin : margin + inner]
+        left_ref[c] = total[:, :margin].astype(left_ref.dtype)
+        right_ref[c] = total[:, margin + inner :].astype(right_ref.dtype)
+
+
+def local_gradient(tile, before, after, probe, rows_list, cols_list, amplitudes):
+    channels, high, inner = tile.shape
+    margin = before.shape[2]
     size = probe.shape[-1]
     probes = amplitudes.shape[0]
     chunk = 4 if probes % 4 == 0 else 2
     tables = jnp.asarray(operator_tables(size))
     smem = pl.BlockSpec(memory_space=pltpu.SMEM)
     vmem = pl.BlockSpec(memory_space=pltpu.VMEM)
-    out = pl.pallas_call(
+    padded = pltpu.VMEM((channels, high, inner + 2 * margin), jnp.float32)
+    edge = jax.ShapeDtypeStruct(before.shape, jnp.bfloat16)
+    return pl.pallas_call(
         lambda *refs: wave_kernel(size, chunk, *refs),
-        out_shape=jax.ShapeDtypeStruct((layers * parts, high, wide), jnp.float32),
-        in_specs=[smem, smem, vmem, vmem, vmem, vmem],
-        out_specs=vmem,
+        out_shape=(jax.ShapeDtypeStruct(tile.shape, jnp.float32), edge, edge),
+        in_specs=[smem, smem] + [vmem] * 6,
+        out_specs=(vmem, vmem, vmem),
+        scratch_shapes=[padded, padded],
         name="waves",
-    )(
-        rows_list.reshape(1, -1),
-        cols_list.reshape(1, -1),
-        padded.reshape(layers * parts, high, wide),
-        probe,
-        amplitudes,
-        tables,
-    )
-    return out.reshape(layers, parts, high, wide)
+    )(rows_list.reshape(1, -1), cols_list.reshape(1, -1), tile, before, after, probe, amplitudes, tables)
 
 
 MESH = pl.DeviceIdType.MESH
@@ -230,7 +220,7 @@
     lax.fori_loop(1, lax.axis_size("tile"), wait, 0)
 
 
-def fetch_kernel(across, rows, direct, extra, got, near, near_sum, run, run_sum, far,
+def fetch_kernel(across, rows, ids, second_ids, second_valid, blocks, got, direct, extra, near, near_sum, run, run_sum, far,
                  own_sem, send_sem, recv_sem, hop_send, hop_recv):
     count = lax.axis_size("tile")
     core, col, row = place(lax.axis_index("tile"), across)
@@ -240,6 +230,17 @@
             src_ref=source, dst_ref=target, send_sem=hop_send.at[k], recv_sem=hop_recv.at[k],
             device_id={"tile": tile}, device_id_type=MESH)
 
+    def fill_extra(e, carry):
+        block = jnp.where(second_valid[0, e] > 0, blocks[second_ids[0, e]], 0.0)
+        extra[e // (across * rows), e // rows % across, e % rows] = block.astype(extra.dtype)
+        return carry
+
+    def fill_direct(t, carry):
+        direct[t] = blocks[ids[0, t]].astype(direct.dtype)
+        return carry
+
+    lax.fori_loop(0, count, fill_extra, 0)
+    lax.fori_loop(0, count, fill_direct, 0)
     greet("tile")
     first = hop(0, extra.at[1 - core], near, (row * across + col) * 2 + 1 - core)
     first.start()
@@ -332,22 +333,26 @@
     return [dma, dma((count,)), dma((count,)), dma((across + rows,)), dma((across + rows,))]
 
 
-def fetch(direct, extra):
-    count, high, wide = direct.shape
+def fetch(blocks, ids, second_ids, second_valid):
+    high, wide = blocks.shape[1:]
+    count = ids.shape[0]
+    scalars = [x.reshape(1, count).astype(jnp.int32) for x in (ids, second_ids, second_valid)]
     across, rows = chips_of(count)
+    smem = pl.BlockSpec(memory_space=pltpu.SMEM)
     vmem = pl.BlockSpec(memory_space=pltpu.VMEM)
-    buffer = lambda *dims: pltpu.VMEM((*dims, high, wide), direct.dtype)
+    buffer = lambda *dims: pltpu.VMEM((*dims, high, wide), jnp.bfloat16)
     return pl.pallas_call(
         lambda *refs: fetch_kernel(across, rows, *refs),
-        out_shape=jax.ShapeDtypeStruct((count + 1, high, wide), direct.dtype),
-        in_specs=[vmem, vmem],
+        out_shape=jax.ShapeDtypeStruct((count + 1, high, wide), jnp.bfloat16),
+        in_specs=[smem, smem, smem, vmem],
         out_specs=vmem,
         scratch_shapes=[
+            buffer(count), buffer(2, across, rows),
             buffer(across, rows), buffer(across, rows), buffer(across - 1, rows),
             buffer(rows), buffer(rows - 1), *exchange_sems(count, across, rows)],
         compiler_params=pltpu.CompilerParams(collective_id=1, has_side_effects=True),
         name="fetch",
-    )(direct, extra)
+    )(*scalars, blocks)
 
 
 def give_back(direct, extra):
@@ -505,15 +510,15 @@
     send_valid = jnp.stack([last_slot >= 0, last_slot > first_slot], axis=1)
     chosen = slots[:, :, None] == request_slots[None, None, :]
     send_block = jnp.sum(jnp.where(chosen, group_block[:, None, :], 0), axis=2)
-    blocks = volume.astype(jnp.bfloat16)
     weight = interp_weights[0, 0]
     complement = 1.0 - weight
     block_size = (2 * block_rows, slab_width)
-    flat = blocks.reshape(block_count, *block_size)
-    extra_out = jnp.where(
-        by_core(send_valid[:, 1])[..., None, None], flat[by_core(send_block[:, 1])], 0
-    ).astype(jnp.bfloat16)
-    incoming = fetch(flat[send_block[:, 0]], extra_out)
+    incoming = fetch(
+        volume.reshape(block_count, *block_size),
+        send_block[:, 0],
+        by_core(send_block[:, 1]),
+        by_core(send_valid[:, 1]),
+    )
     fetched = (
         incoming[jnp.where(my_rank == 0, my_owner, tile_count)]
         .astype(jnp.float32)
@@ -527,14 +532,16 @@
         0, 2, 1, 3, 4
     )
     object_tile = object_tile.reshape(layers, 2, slab_width, slab_width).astype(jnp.bfloat16)
-    padded = with_halo(object_tile, (("tile", 3),), margin).astype(jnp.float32)
-    grad_padded = local_gradient(padded, probe, scan_rows[0, 0], scan_cols[0, 0], measured[0, 0])
-    edges = grad_padded.astype(jnp.bfloat16)
-    from_left = from_behind(edges[..., margin + slab_width :], "tile", 1).astype(jnp.float32)
-    from_right = from_behind(edges[..., :margin], "tile", -1).astype(jnp.float32)
-    interior = grad_padded[..., margin : margin + slab_width]
-    middle = jnp.zeros((layers, 2, slab_width, slab_width - 2 * margin), jnp.float32)
-    interior = interior + jnp.concatenate([from_left, middle, from_right], axis=3)
+    object_tile = object_tile.reshape(layers * 2, slab_width, slab_width)
+    before = from_behind(object_tile[..., slab_width - margin :], "tile", 1)
+    after = from_behind(object_tile[..., :margin], "tile", -1)
+    interior, low_edge, high_edge = local_gradient(
+        object_tile, before, after, probe, scan_rows[0, 0], scan_cols[0, 0], measured[0, 0]
+    )
+    from_left = from_behind(high_edge, "tile", 1).astype(jnp.float32)
+    from_right = from_behind(low_edge, "tile", -1).astype(jnp.float32)
+    middle = jnp.zeros((layers * 2, slab_width, slab_width - 2 * margin), jnp.float32)
+    interior = interior + jnp.concatenate([from_left, middle, from_right], axis=2)
     grad_rows = interior.reshape(layers, 2, per_slice, block_rows, slab_width).transpose(
         0, 2, 1, 3, 4
     )

time: 177 us -> 175 us (0.989)
  other arithmetic: 12.8 us -> 7.87 us
  waiting for transfers between devices: 4.72 us -> 6.96 us
  Pallas kernels: 132 us -> 134 us
    ppermute x2 -> x4, waiting for transfers between devices: 0.93 us -> 6.96 us  [from_behind(): return lax.ppermute(array, axis, pairs)]
    ppermute x2 -> x0, starting transfers between devices: 5.56 us -> none  [the longest x1 3.64 us: with_halo(): lax.ppermute(head, axis, [((i + 1) % count, i) for i in range(ends)])]
    ppermute x2 -> x4, starting transfers between devices: 5.86 us -> 10 us  [from_behind(): return lax.ppermute(array, axis, pairs)]
    convert_element_type x5 -> x3, other arithmetic: 4.21 us -> 0.08 us  [the longest x1 0.04 us: per_device(): from_left = from_behind(high_edge, 'tile', 1).astype(jnp.float32)]
    ppermute x2 -> x0, waiting for transfers between devices: 3.8 us -> none  [the longest x1 2.04 us: with_halo(): lax.ppermute(tail, axis, [(i, (i + 1) % count) for i in range(ends)])]
    gather x2 -> x0, local copies, waits for them, and re-layouts: 2.26 us -> none  [the longest x1 1.64 us: per_device(): incoming = fetch(flat[send_block[:, 0]], extra_out)]
where the time goes in v5:
time: 175 us
  Pallas kernels  134 us (77%)
  starting transfers between devices  10 us (6%)
  local copies, waits for them, and re-layouts  9.94 us (6%)
  other arithmetic  7.87 us (4%)
  waiting for transfers between devices  6.96 us (4%)
  matrix products  2.92 us (2%)
  between operations  2.9 us (2%)
    pallas_call x1, Pallas kernels, give_back(): pl.pallas_call(lambda *refs: return_kernel(across, rows, *refs), out_shap...  41.7 us
    pallas_call x1, Pallas kernels, sum_over_angle(): pl.pallas_call(angle_kernel, out_shape=jax.ShapeDtypeStruct((ring, 2, hig...  40 us
    pallas_call x1, Pallas kernels, fetch(): pl.pallas_call(lambda *refs: fetch_kernel(across, rows, *refs), out_shape...  39.5 us
    pallas_call x1, Pallas kernels, local_gradient(): pl.pallas_call(lambda *refs: wave_kernel(size, chunk, *refs), out_shape=(...  12.9 us
    ppermute x4, starting transfers between devices, from_behind(): return lax.ppermute(array, axis, pairs)  10 us
    ppermute x4, waiting for transfers between devices, from_behind(): return lax.ppermute(array, axis, pairs)  6.96 us
  transfers between devices with their start and end apart: 4, of which 3 were waited for; matrix products, arithmetic and copies ran while one was open for 1% of the time, Pallas kernels for 0%

profile of v5, /device:TPU:14, one launch (start us, length us, event | category | flops | bytes accessed | tf_op | source)
XLA Modules:
  0.0 174.8 jit_solution(2337519848800142556)
XLA Ops:
  0.6 0.5 broadcast.121
  1.1 1.3 reduce.7
  2.5 0.1 mul.89
  2.5 0.8 select_reduce_fusion.3
  3.4 0.7 fusion.19
  4.1 0.2 convert_reduce_fusion
  4.3 0.1 select_reduce_fusion.1
  4.4 0.7 fusion.17
  5.1 0.9 select_reduce_fusion
  6.0 0.5 slice_reduce_fusion
  6.5 0.1 reshape_squeeze.19
  6.6 0.1 copy.48
  6.7 0.6 reshape.164.refs_1_
  7.4 0.1 reshape.170
  7.4 0.1 copy.49
  7.6 0.6 reshape.168.refs_2_
  8.2 39.5 %fetch.1 = bf16[33,64,256]{2,1,0:T(8,128)(2,1)} custom-call(s32[1,32]{1,0:T(1,128)} %get-tuple-element.23.refs_0_, s32[1,32]{1,0:T(1,128)} %reshape.164.refs_1_, s32[1,32]{1,0:T(1,128)} %reshape.168.refs_2_, f32[8,64,256]{2,1,0:T(8,128)} %bitcast.93), custom_call_target="tpu_custom_call" | custom-call | tf_op jit(solution)/shard_map/fetch/pallas_call | solution.py:344
  47.7 1.9 %gather_fusion = bf16[32,64,256]{2,1,0:T(8,128)(2,1)S(1)} fusion(bf16[33,64,256]{2,1,0:T(8,128)(2,1)} %fetch.1, s32[1024]{0:T(1024)S(1)} %pad_clamp_fusion.1), kind=kCustom, calls=%fused_computation | custom fusion | bytes 2097280 | tf_op jit(solution)/shard_map/gather | solution.py:523
  49.5 0.3 fusion.22
  49.8 0.0 copy-start.7
  49.8 0.2 fusion.10
  50.1 0.0 copy-start
  50.1 0.1 fusion.23
  50.2 1.9 %collective-permute-start.1 = (bf16[4,256,64]{2,1,0:T(8,128)(2,1)S(1)}, bf16[4,256,64]{2,1,0:T(8,128)(2,1)S(1)}, u32[]{:S(2)}, u32[]{:S(2)}) collective-permute-start(bf16[4,256,64]{2,1,0:T(8,128)(2,1)S(1)} %get-tuple-element.18), channel_id=1, source_target_pairs={{1,0},{2,1},{3,2},{4,3},{5,4},{6,5},{7,6},{8,7},{9,8},{10,9},{11,1... | collective-permute-start | bytes 393224 | tf_op jit(solution)/shard_map/ppermute | solution.py:22
  52.2 2.4 %collective-permute-start = (bf16[4,256,64]{2,1,0:T(8,128)(2,1)S(1)}, bf16[4,256,64]{2,1,0:T(8,128)(2,1)S(1)}, u32[]{:S(2)}, u32[]{:S(2)}) collective-permute-start(bf16[4,256,64]{2,1,0:T(8,128)(2,1)S(1)} %get-tuple-element.19), channel_id=1, source_target_pairs={{0,1},{1,2},{2,3},{3,4},{4,5},{5,6},{6,7},{7,8},{8,9},{9,10},{10,1... | collective-permute-start | bytes 393224 | tf_op jit(solution)/shard_map/ppermute | solution.py:22
  54.6 0.0 copy-done.7
  54.7 1.4 collective-permute-done.1.refs_4_
  56.0 0.0 copy-start.5
  56.0 3.8 %collective-permute-done.refs_3_ = bf16[4,256,64]{2,1,0:T(8,128)(2,1)S(1)} collective-permute-done((bf16[4,256,64]{2,1,0:T(8,128)(2,1)S(1)}, bf16[4,256,64]{2,1,0:T(8,128)(2,1)S(1)}, u32[]{:S(2)}, u32[]{:S(2)}) %collective-permute-start) | collective-permute-done | bytes 131104 | tf_op jit(solution)/shard_map/ppermute | solution.py:22
  59.9 0.0 copy-start.6
  59.9 0.0 copy-done
  59.9 0.0 copy-done.5
  59.9 0.7 copy-done.6
  60.6 12.9 %waves.1 = (f32[4,256,256]{2,1,0:T(8,128)}, bf16[4,256,64]{2,1,0:T(8,128)(2,1)}, bf16[4,256,64]{2,1,0:T(8,128)(2,1)}) custom-call(s32[1,8]{1,0:T(1,128)} %bitcast.103, s32[1,8]{1,0:T(1,128)} %bitcast.104, bf16[4,256,256]{2,1,0:T(8,128)(2,1)} %bitcast.87, bf16[4,256,64]{2,1,0:T(8,128)(2,1)} %copy-done.6, bf16[4,256,64]{2,1,0:T(8,128)(2,1)} %copy-done.5, ...), custom_call_target="tpu_custom_call" | custom-call | tf_op jit(solution)/shard_map/waves/pallas_call | solution.py:154
  73.5 0.0 copy-start.2
  73.5 2.7 %collective-permute-start.2 = (bf16[4,256,64]{2,1,0:T(8,128)(2,1)}, bf16[4,256,64]{2,1,0:T(8,128)(2,1)S(1)}, u32[]{:S(2)}, u32[]{:S(2)}) collective-permute-start(bf16[4,256,64]{2,1,0:T(8,128)(2,1)} %get-tuple-element.7), channel_id=1, source_target_pairs={{0,1},{1,2},{2,3},{3,4},{4,5},{5,6},{6,7},{7,8},{8,9},{9,10},{10,1... | collective-permute-start | bytes 393224 | tf_op jit(solution)/shard_map/ppermute | solution.py:22
  76.2 3.0 %collective-permute-start.3 = (bf16[4,256,64]{2,1,0:T(8,128)(2,1)}, bf16[4,256,64]{2,1,0:T(8,128)(2,1)S(1)}, u32[]{:S(2)}, u32[]{:S(2)}) collective-permute-start(bf16[4,256,64]{2,1,0:T(8,128)(2,1)} %get-tuple-element.8), channel_id=1, source_target_pairs={{1,0},{2,1},{3,2},{4,3},{5,4},{6,5},{7,6},{8,7},{9,8},{10,9},{11,1... | collective-permute-start | bytes 393224 | tf_op jit(solution)/shard_map/ppermute | solution.py:22
  79.2 0.6 fusion.16
  81.1 0.1 copy.45
  81.3 0.1 copy.47
  82.0 0.1 pad.3.clone
  82.1 0.0 collective-permute-done.2
  82.1 1.8 %collective-permute-done.3 = bf16[4,256,64]{2,1,0:T(8,128)(2,1)S(1)} collective-permute-done((bf16[4,256,64]{2,1,0:T(8,128)(2,1)}, bf16[4,256,64]{2,1,0:T(8,128)(2,1)S(1)}, u32[]{:S(2)}, u32[]{:S(2)}) %collective-permute-start.3) | collective-permute-done | bytes 131104 | tf_op jit(solution)/shard_map/ppermute | solution.py:22
  84.0 0.0 copy-done.2
  84.0 0.2 maximum_add_fusion
  84.2 0.1 copy.53
  84.3 0.2 fusion.7
  84.5 0.1 pad_maximum_fusion
  84.6 0.1 copy.54
  84.7 0.6 dynamic-slice_bitcast_fusion.refs_1_
  85.3 1.6 gather_fusion.1
  86.9 41.7 %give_back.1 = bf16[64,64,256]{2,1,0:T(8,128)(2,1)} custom-call(bf16[32,64,256]{2,1,0:T(8,128)(2,1)} %gather_fusion.1, bf16[64,256]{1,0:T(8,128)(2,1)} %dynamic-slice_bitcast_fusion.refs_1_), custom_call_target="tpu_custom_call" | custom-call | tf_op jit(solution)/shard_map/give_back/pallas_call | solution.py:362
  128.6 0.0 copy-start.1
  128.6 0.0 copy-start.3
  128.6 0.0 copy-start.4
  128.7 2.9 %fusion.2 = bf16[8,64,256]{2,0,1:T(8,128)(2,1)S(1)} fusion(bf16[64,64,256]{2,1,0:T(8,128)(2,1)} %give_back.1, pred[32,8]{0,1:T(8,128)(4,1)S(1)} %copy.47, pred[32,8]{0,1:T(8,128)(4,1)S(1)} %get-tuple-element.20), kind=kOutput, calls=%fused_computation.4 | convolution fusion | flops 16908800 | bytes 2359808 | tf_op jit(solution)/shard_map/nb,nhw->bhw/dot_general | solution.py:568
  131.6 0.8 copy.56
  132.3 40.0 %angle_sum.1 = f32[8,2,32,256]{3,2,1,0:T(8,128)} custom-call(bf16[8,2,32,256]{3,2,1,0:T(8,128)(2,1)} %bitcast.94), custom_call_target="tpu_custom_call" | custom-call | tf_op jit(solution)/shard_map/angle_sum/pallas_call | solution.py:453
  172.4 0.0 copy-done.1
  172.4 0.0 copy-done.3
  172.4 0.0 copy-done.4
  172.4 2.4 %divide_subtract_fusion = (f32[8,2,32,256]{3,2,1,0:T(8,128)}, f32[8,2,32,256]{3,2,1,0:T(8,128)}, f32[8,2,32,256]{3,2,1,0:T(8,128)}) fusion(f32[8,2,32,256]{3,2,1,0:T(8,128)S(1)} %copy-done.1, f32[8,2,32,256]{3,2,1,0:T(8,128)} %angle_sum.1, f32[8,2,32,256]{3,2,1,0:T(8,128)S(1)} %copy-done.3, f32[8,2,32,256]{3,2,1,0:T(8,128)S(1)} %copy-done.4), kind=kLoop, calls=%fused_computation.18 | loop fusion | flops 1441792 | bytes 3670016 | tf_op jit(solution)/shard_map/sub | solution.py:473
  (17 shorter events, 0.2 us)
Async XLA Ops:
  49.8 4.8 %copy-start.7 = (f32[1,1,16]{2,1,0:T(1,128)S(1)}, f32[1,1,16]{2,1,0:T(1,128)}, u32[]{:S(2)}) copy-start(f32[1,1,16]{2,1,0:T(1,128)} %param.20) | copy-start | bytes 196
  50.1 9.8 %copy-start = (bf16[2,2,8,32,256]{4,3,2,1,0:T(8,128)(2,1)}, bf16[2,2,8,32,256]{4,3,2,1,0:T(8,128)(2,1)S(1)}, u32[]{:S(2)}) copy-start(bf16[2,2,8,32,256]{4,3,2,1,0:T(8,128)(2,1)S(1)} %copy.52) | copy-start | bytes 1572868
  50.2 5.8 %collective-permute-start.1 = (bf16[4,256,64]{2,1,0:T(8,128)(2,1)S(1)}, bf16[4,256,64]{2,1,0:T(8,128)(2,1)S(1)}, u32[]{:S(2)}, u32[]{:S(2)}) collective-permute-start(bf16[4,256,64]{2,1,0:T(8,128)(2,1)S(1)} %get-tuple-element.18), channel_id=1, source_target_pairs={{1,0},{2,1},{3,2},{4,3},{5,4},{6,5},{7,6},{8,7},{9,8},{10,9},{11,1... | collective-permute-start | bytes 393224 | tf_op jit(solution)/shard_map/ppermute | solution.py:22
  52.2 7.7 %collective-permute-start = (bf16[4,256,64]{2,1,0:T(8,128)(2,1)S(1)}, bf16[4,256,64]{2,1,0:T(8,128)(2,1)S(1)}, u32[]{:S(2)}, u32[]{:S(2)}) collective-permute-start(bf16[4,256,64]{2,1,0:T(8,128)(2,1)S(1)} %get-tuple-element.19), channel_id=1, source_target_pairs={{0,1},{1,2},{2,3},{3,4},{4,5},{5,6},{6,7},{7,8},{8,9},{9,10},{10,1... | collective-permute-start | bytes 393224 | tf_op jit(solution)/shard_map/ppermute | solution.py:22
  56.0 3.8 %copy-start.5 = (bf16[4,256,64]{2,1,0:T(8,128)(2,1)}, bf16[4,256,64]{2,1,0:T(8,128)(2,1)S(1)}, u32[]{:S(2)}) copy-start(bf16[4,256,64]{2,1,0:T(8,128)(2,1)S(1)} %collective-permute-done.1.refs_4_) | copy-start | bytes 393220
  59.9 0.7 copy-start.6
  73.5 10.4 %copy-start.2 = (f32[4,256,256]{2,1,0:T(8,128)S(1)}, f32[4,256,256]{2,1,0:T(8,128)}, u32[]{:S(2)}) copy-start(f32[4,256,256]{2,1,0:T(8,128)} %get-tuple-element.6) | copy-start | bytes 3145732
  73.5 8.6 %collective-permute-start.2 = (bf16[4,256,64]{2,1,0:T(8,128)(2,1)}, bf16[4,256,64]{2,1,0:T(8,128)(2,1)S(1)}, u32[]{:S(2)}, u32[]{:S(2)}) collective-permute-start(bf16[4,256,64]{2,1,0:T(8,128)(2,1)} %get-tuple-element.7), channel_id=1, source_target_pairs={{0,1},{1,2},{2,3},{3,4},{4,5},{5,6},{6,7},{7,8},{8,9},{9,10},{10,1... | collective-permute-start | bytes 393224 | tf_op jit(solution)/shard_map/ppermute | solution.py:22
  76.2 7.7 %collective-permute-start.3 = (bf16[4,256,64]{2,1,0:T(8,128)(2,1)}, bf16[4,256,64]{2,1,0:T(8,128)(2,1)S(1)}, u32[]{:S(2)}, u32[]{:S(2)}) collective-permute-start(bf16[4,256,64]{2,1,0:T(8,128)(2,1)} %get-tuple-element.8), channel_id=1, source_target_pairs={{1,0},{2,1},{3,2},{4,3},{5,4},{6,5},{7,6},{8,7},{9,8},{10,9},{11,1... | collective-permute-start | bytes 393224 | tf_op jit(solution)/shard_map/ppermute | solution.py:22
  128.6 43.7 %copy-start.1 = (f32[8,2,32,256]{3,2,1,0:T(8,128)S(1)}, f32[8,2,32,256]{3,2,1,0:T(8,128)}, u32[]{:S(2)}) copy-start(f32[8,2,32,256]{3,2,1,0:T(8,128)} %param.11) | copy-start | bytes 1572868
  128.6 43.7 %copy-start.3 = (f32[8,2,32,256]{3,2,1,0:T(8,128)S(1)}, f32[8,2,32,256]{3,2,1,0:T(8,128)}, u32[]{:S(2)}) copy-start(f32[8,2,32,256]{3,2,1,0:T(8,128)} %param.12) | copy-start | bytes 1572868
  128.6 43.7 %copy-start.4 = (f32[8,2,32,256]{3,2,1,0:T(8,128)S(1)}, f32[8,2,32,256]{3,2,1,0:T(8,128)}, u32[]{:S(2)}) copy-start(f32[8,2,32,256]{3,2,1,0:T(8,128)} %param.13) | copy-start | bytes 1572868

commit v6 on v5

--- a/solution.py
+++ b/solution.py
@@ -198,7 +198,11 @@
 
 
 def start_direct(first, last, source, target, send_sem, recv_sem):
-    def start(d, carry):
+    count = lax.axis_size("tile")
+    skip = 2 * chips_of(count)[0] - 1
+
+    def start(k, carry):
+        d = lax.rem(k - 1 + skip, count - 1) + 1
         direct_copy(d, source, target, send_sem, recv_sem).start()
         return carry
 

time: 175 us -> 175 us (level)
  no operation moved by 1% of the time
where the time goes in v6:
time: 175 us; the launch traced here: 174 us
  Pallas kernels  134 us (77%)
  starting transfers between devices  10 us (6%)
  local copies, waits for them, and re-layouts  9.94 us (6%)
  other arithmetic  7.87 us (4%)
  waiting for transfers between devices  7.25 us (4%)
  matrix products  2.92 us (2%)
  between operations  2.9 us (2%)
    pallas_call x1, Pallas kernels, give_back(): pl.pallas_call(lambda *refs: return_kernel(across, rows, *refs), out_shap...  41.5 us
    pallas_call x1, Pallas kernels, sum_over_angle(): pl.pallas_call(angle_kernel, out_shape=jax.ShapeDtypeStruct((ring, 2, hig...  40.7 us
    pallas_call x1, Pallas kernels, fetch(): pl.pallas_call(lambda *refs: fetch_kernel(across, rows, *refs), out_shape...  38.4 us
    pallas_call x1, Pallas kernels, local_gradient(): pl.pallas_call(lambda *refs: wave_kernel(size, chunk, *refs), out_shape=(...  12.9 us
    ppermute x4, starting transfers between devices, from_behind(): return lax.ppermute(array, axis, pairs)  10 us
    ppermute x4, waiting for transfers between devices, from_behind(): return lax.ppermute(array, axis, pairs)  7.25 us
  transfers between devices with their start and end apart: 4, of which 3 were waited for; matrix products, arithmetic and copies ran while one was open for 1% of the time, Pallas kernels for 0%

profile of v6, /device:TPU:14, one launch (start us, length us, event | category | flops | bytes accessed | tf_op | source)
XLA Modules:
  0.0 174.4 jit_solution(12366621636300319378)
XLA Ops:
  0.6 0.5 broadcast.121
  1.1 1.3 reduce.7
  2.5 0.1 mul.89
  2.5 0.8 select_reduce_fusion.3
  3.4 0.7 fusion.19
  4.1 0.2 convert_reduce_fusion
  4.3 0.1 select_reduce_fusion.1
  4.4 0.7 fusion.17
  5.1 0.9 select_reduce_fusion
  6.0 0.5 slice_reduce_fusion
  6.5 0.1 reshape_squeeze.19
  6.6 0.1 copy.48
  6.7 0.6 reshape.164.refs_1_
  7.4 0.1 reshape.170
  7.4 0.1 copy.49
  7.6 0.6 reshape.168.refs_2_
  8.2 38.4 %fetch.1 = bf16[33,64,256]{2,1,0:T(8,128)(2,1)} custom-call(s32[1,32]{1,0:T(1,128)} %get-tuple-element.23.refs_0_, s32[1,32]{1,0:T(1,128)} %reshape.164.refs_1_, s32[1,32]{1,0:T(1,128)} %reshape.168.refs_2_, f32[8,64,256]{2,1,0:T(8,128)} %bitcast.93), custom_call_target="tpu_custom_call" | custom-call | tf_op jit(solution)/shard_map/fetch/pallas_call | solution.py:348
  46.6 1.9 %gather_fusion = bf16[32,64,256]{2,1,0:T(8,128)(2,1)S(1)} fusion(bf16[33,64,256]{2,1,0:T(8,128)(2,1)} %fetch.1, s32[1024]{0:T(1024)S(1)} %pad_clamp_fusion.1), kind=kCustom, calls=%fused_computation | custom fusion | bytes 2097280 | tf_op jit(solution)/shard_map/gather | solution.py:527
  48.5 0.3 fusion.22
  48.8 0.0 copy-start.7
  48.8 0.2 fusion.10
  49.0 0.0 copy-start
  49.0 0.1 fusion.23
  49.2 1.9 %collective-permute-start.1 = (bf16[4,256,64]{2,1,0:T(8,128)(2,1)S(1)}, bf16[4,256,64]{2,1,0:T(8,128)(2,1)S(1)}, u32[]{:S(2)}, u32[]{:S(2)}) collective-permute-start(bf16[4,256,64]{2,1,0:T(8,128)(2,1)S(1)} %get-tuple-element.18), channel_id=1, source_target_pairs={{1,0},{2,1},{3,2},{4,3},{5,4},{6,5},{7,6},{8,7},{9,8},{10,9},{11,1... | collective-permute-start | bytes 393224 | tf_op jit(solution)/shard_map/ppermute | solution.py:22
  51.1 2.4 %collective-permute-start = (bf16[4,256,64]{2,1,0:T(8,128)(2,1)S(1)}, bf16[4,256,64]{2,1,0:T(8,128)(2,1)S(1)}, u32[]{:S(2)}, u32[]{:S(2)}) collective-permute-start(bf16[4,256,64]{2,1,0:T(8,128)(2,1)S(1)} %get-tuple-element.19), channel_id=1, source_target_pairs={{0,1},{1,2},{2,3},{3,4},{4,5},{5,6},{6,7},{7,8},{8,9},{9,10},{10,1... | collective-permute-start | bytes 393224 | tf_op jit(solution)/shard_map/ppermute | solution.py:22
  53.6 0.0 copy-done.7
  53.6 1.4 collective-permute-done.1.refs_4_
  55.0 0.0 copy-start.5
  55.0 3.8 %collective-permute-done.refs_3_ = bf16[4,256,64]{2,1,0:T(8,128)(2,1)S(1)} collective-permute-done((bf16[4,256,64]{2,1,0:T(8,128)(2,1)S(1)}, bf16[4,256,64]{2,1,0:T(8,128)(2,1)S(1)}, u32[]{:S(2)}, u32[]{:S(2)}) %collective-permute-start) | collective-permute-done | bytes 131104 | tf_op jit(solution)/shard_map/ppermute | solution.py:22
  58.8 0.0 copy-start.6
  58.8 0.0 copy-done
  58.8 0.0 copy-done.5
  58.8 0.7 copy-done.6
  59.5 12.9 %waves.1 = (f32[4,256,256]{2,1,0:T(8,128)}, bf16[4,256,64]{2,1,0:T(8,128)(2,1)}, bf16[4,256,64]{2,1,0:T(8,128)(2,1)}) custom-call(s32[1,8]{1,0:T(1,128)} %bitcast.103, s32[1,8]{1,0:T(1,128)} %bitcast.104, bf16[4,256,256]{2,1,0:T(8,128)(2,1)} %bitcast.87, bf16[4,256,64]{2,1,0:T(8,128)(2,1)} %copy-done.6, bf16[4,256,64]{2,1,0:T(8,128)(2,1)} %copy-done.5, ...), custom_call_target="tpu_custom_call" | custom-call | tf_op jit(solution)/shard_map/waves/pallas_call | solution.py:154
  72.5 0.0 copy-start.2
  72.5 3.0 %collective-permute-start.2 = (bf16[4,256,64]{2,1,0:T(8,128)(2,1)}, bf16[4,256,64]{2,1,0:T(8,128)(2,1)S(1)}, u32[]{:S(2)}, u32[]{:S(2)}) collective-permute-start(bf16[4,256,64]{2,1,0:T(8,128)(2,1)} %get-tuple-element.7), channel_id=1, source_target_pairs={{0,1},{1,2},{2,3},{3,4},{4,5},{5,6},{6,7},{7,8},{8,9},{9,10},{10,1... | collective-permute-start | bytes 393224 | tf_op jit(solution)/shard_map/ppermute | solution.py:22
  75.4 2.7 %collective-permute-start.3 = (bf16[4,256,64]{2,1,0:T(8,128)(2,1)}, bf16[4,256,64]{2,1,0:T(8,128)(2,1)S(1)}, u32[]{:S(2)}, u32[]{:S(2)}) collective-permute-start(bf16[4,256,64]{2,1,0:T(8,128)(2,1)} %get-tuple-element.8), channel_id=1, source_target_pairs={{1,0},{2,1},{3,2},{4,3},{5,4},{6,5},{7,6},{8,7},{9,8},{10,9},{11,1... | collective-permute-start | bytes 393224 | tf_op jit(solution)/shard_map/ppermute | solution.py:22
  78.2 0.6 fusion.16
  80.1 0.1 copy.45
  80.2 0.1 copy.47
  81.0 0.1 pad.3.clone
  81.0 0.0 collective-permute-done.2
  81.1 2.0 %collective-permute-done.3 = bf16[4,256,64]{2,1,0:T(8,128)(2,1)S(1)} collective-permute-done((bf16[4,256,64]{2,1,0:T(8,128)(2,1)}, bf16[4,256,64]{2,1,0:T(8,128)(2,1)S(1)}, u32[]{:S(2)}, u32[]{:S(2)}) %collective-permute-start.3) | collective-permute-done | bytes 131104 | tf_op jit(solution)/shard_map/ppermute | solution.py:22
  83.2 0.0 copy-done.2
  83.2 0.2 maximum_add_fusion
  83.4 0.1 copy.53
  83.5 0.2 fusion.7
  83.7 0.1 pad_maximum_fusion
  83.8 0.1 copy.54
  83.9 0.6 dynamic-slice_bitcast_fusion.refs_1_
  84.6 1.6 gather_fusion.1
  86.1 41.5 %give_back.1 = bf16[64,64,256]{2,1,0:T(8,128)(2,1)} custom-call(bf16[32,64,256]{2,1,0:T(8,128)(2,1)} %gather_fusion.1, bf16[64,256]{1,0:T(8,128)(2,1)} %dynamic-slice_bitcast_fusion.refs_1_), custom_call_target="tpu_custom_call" | custom-call | tf_op jit(solution)/shard_map/give_back/pallas_call | solution.py:366
  127.6 0.0 copy-start.1
  127.6 0.0 copy-start.3
  127.7 0.0 copy-start.4
  127.7 2.9 %fusion.2 = bf16[8,64,256]{2,0,1:T(8,128)(2,1)S(1)} fusion(bf16[64,64,256]{2,1,0:T(8,128)(2,1)} %give_back.1, pred[32,8]{0,1:T(8,128)(4,1)S(1)} %copy.47, pred[32,8]{0,1:T(8,128)(4,1)S(1)} %get-tuple-element.20), kind=kOutput, calls=%fused_computation.4 | convolution fusion | flops 16908800 | bytes 2359808 | tf_op jit(solution)/shard_map/nb,nhw->bhw/dot_general | solution.py:572
  130.6 0.8 copy.56
  131.3 40.7 %angle_sum.1 = f32[8,2,32,256]{3,2,1,0:T(8,128)} custom-call(bf16[8,2,32,256]{3,2,1,0:T(8,128)(2,1)} %bitcast.94), custom_call_target="tpu_custom_call" | custom-call | tf_op jit(solution)/shard_map/angle_sum/pallas_call | solution.py:457
  172.0 0.0 copy-done.1
  172.0 0.0 copy-done.3
  172.0 0.0 copy-done.4
  172.0 2.4 %divide_subtract_fusion = (f32[8,2,32,256]{3,2,1,0:T(8,128)}, f32[8,2,32,256]{3,2,1,0:T(8,128)}, f32[8,2,32,256]{3,2,1,0:T(8,128)}) fusion(f32[8,2,32,256]{3,2,1,0:T(8,128)S(1)} %copy-done.1, f32[8,2,32,256]{3,2,1,0:T(8,128)} %angle_sum.1, f32[8,2,32,256]{3,2,1,0:T(8,128)S(1)} %copy-done.3, f32[8,2,32,256]{3,2,1,0:T(8,128)S(1)} %copy-done.4), kind=kLoop, calls=%fused_computation.18 | loop fusion | flops 1441792 | bytes 3670016 | tf_op jit(solution)/shard_map/sub | solution.py:477
  (17 shorter events, 0.2 us)
Async XLA Ops:
  48.8 4.8 %copy-start.7 = (f32[1,1,16]{2,1,0:T(1,128)S(1)}, f32[1,1,16]{2,1,0:T(1,128)}, u32[]{:S(2)}) copy-start(f32[1,1,16]{2,1,0:T(1,128)} %param.20) | copy-start | bytes 196
  49.0 9.8 %copy-start = (bf16[2,2,8,32,256]{4,3,2,1,0:T(8,128)(2,1)}, bf16[2,2,8,32,256]{4,3,2,1,0:T(8,128)(2,1)S(1)}, u32[]{:S(2)}) copy-start(bf16[2,2,8,32,256]{4,3,2,1,0:T(8,128)(2,1)S(1)} %copy.52) | copy-start | bytes 1572868
  49.2 5.8 %collective-permute-start.1 = (bf16[4,256,64]{2,1,0:T(8,128)(2,1)S(1)}, bf16[4,256,64]{2,1,0:T(8,128)(2,1)S(1)}, u32[]{:S(2)}, u32[]{:S(2)}) collective-permute-start(bf16[4,256,64]{2,1,0:T(8,128)(2,1)S(1)} %get-tuple-element.18), channel_id=1, source_target_pairs={{1,0},{2,1},{3,2},{4,3},{5,4},{6,5},{7,6},{8,7},{9,8},{10,9},{11,1... | collective-permute-start | bytes 393224 | tf_op jit(solution)/shard_map/ppermute | solution.py:22
  51.1 7.7 %collective-permute-start = (bf16[4,256,64]{2,1,0:T(8,128)(2,1)S(1)}, bf16[4,256,64]{2,1,0:T(8,128)(2,1)S(1)}, u32[]{:S(2)}, u32[]{:S(2)}) collective-permute-start(bf16[4,256,64]{2,1,0:T(8,128)(2,1)S(1)} %get-tuple-element.19), channel_id=1, source_target_pairs={{0,1},{1,2},{2,3},{3,4},{4,5},{5,6},{6,7},{7,8},{8,9},{9,10},{10,1... | collective-permute-start | bytes 393224 | tf_op jit(solution)/shard_map/ppermute | solution.py:22
  55.0 3.8 %copy-start.5 = (bf16[4,256,64]{2,1,0:T(8,128)(2,1)}, bf16[4,256,64]{2,1,0:T(8,128)(2,1)S(1)}, u32[]{:S(2)}) copy-start(bf16[4,256,64]{2,1,0:T(8,128)(2,1)S(1)} %collective-permute-done.1.refs_4_) | copy-start | bytes 393220
  58.8 0.7 copy-start.6
  72.5 10.7 %copy-start.2 = (f32[4,256,256]{2,1,0:T(8,128)S(1)}, f32[4,256,256]{2,1,0:T(8,128)}, u32[]{:S(2)}) copy-start(f32[4,256,256]{2,1,0:T(8,128)} %get-tuple-element.6) | copy-start | bytes 3145732
  72.5 8.6 %collective-permute-start.2 = (bf16[4,256,64]{2,1,0:T(8,128)(2,1)}, bf16[4,256,64]{2,1,0:T(8,128)(2,1)S(1)}, u32[]{:S(2)}, u32[]{:S(2)}) collective-permute-start(bf16[4,256,64]{2,1,0:T(8,128)(2,1)} %get-tuple-element.7), channel_id=1, source_target_pairs={{0,1},{1,2},{2,3},{3,4},{4,5},{5,6},{6,7},{7,8},{8,9},{9,10},{10,1... | collective-permute-start | bytes 393224 | tf_op jit(solution)/shard_map/ppermute | solution.py:22
  75.4 7.7 %collective-permute-start.3 = (bf16[4,256,64]{2,1,0:T(8,128)(2,1)}, bf16[4,256,64]{2,1,0:T(8,128)(2,1)S(1)}, u32[]{:S(2)}, u32[]{:S(2)}) collective-permute-start(bf16[4,256,64]{2,1,0:T(8,128)(2,1)} %get-tuple-element.8), channel_id=1, source_target_pairs={{1,0},{2,1},{3,2},{4,3},{5,4},{6,5},{7,6},{8,7},{9,8},{10,9},{11,1... | collective-permute-start | bytes 393224 | tf_op jit(solution)/shard_map/ppermute | solution.py:22
  127.6 44.4 %copy-start.1 = (f32[8,2,32,256]{3,2,1,0:T(8,128)S(1)}, f32[8,2,32,256]{3,2,1,0:T(8,128)}, u32[]{:S(2)}) copy-start(f32[8,2,32,256]{3,2,1,0:T(8,128)} %param.11) | copy-start | bytes 1572868
  127.6 44.4 %copy-start.3 = (f32[8,2,32,256]{3,2,1,0:T(8,128)S(1)}, f32[8,2,32,256]{3,2,1,0:T(8,128)}, u32[]{:S(2)}) copy-start(f32[8,2,32,256]{3,2,1,0:T(8,128)} %param.12) | copy-start | bytes 1572868
  127.7 44.4 %copy-start.4 = (f32[8,2,32,256]{3,2,1,0:T(8,128)S(1)}, f32[8,2,32,256]{3,2,1,0:T(8,128)}, u32[]{:S(2)}) copy-start(f32[8,2,32,256]{3,2,1,0:T(8,128)} %param.13) | copy-start | bytes 1572868
